TPU v7x, 512 devices: a whole 4x8x8 slice. The times are simulated.
512 devices in a mesh: ctx: 64 (over z, y), tp: 8 (over x, core).
Axes of the slice: x: 4, y: 8, z: 8, core: 2. Of those that a mesh axis runs over, the one named last changes fastest.
Arguments:
- query_in: bfloat16 [16384, 2048], P('ctx', 'tp'), may hold values from -6 to 6
- key_in: bfloat16 [16384, 2048], P('ctx', 'tp'), may hold values from -6 to 6
- value_in: bfloat16 [16384, 4096], P('ctx', 'tp'), may hold values from -6 to 6
- gate_values: bfloat16 [16384, 4096], P('ctx', 'tp'), may hold values from -6 to 6
- query_conv: bfloat16 [4, 2048], P(None, 'tp'), may hold values from -3 to 3
- key_conv: bfloat16 [4, 2048], P(None, 'tp'), may hold values from -3 to 3
- value_conv: bfloat16 [4, 4096], P(None, 'tp'), may hold values from -3 to 3
- beta_rate: float32 [32, 16384], P('tp', 'ctx'), may hold values from 0.002 to 0.9, as said below
- log_decay: float32 [32, 16384], P('tp', 'ctx'), may hold values from -0.8 to 0, as said below
- norm_gain: float32 [128], replicated, may hold values from 0.1 to 1.9
- out_weight: bfloat16 [4096, 2048], P('tp'), may hold values from -0.09375 to 0.09375
Outputs:
- layer_out: bfloat16 [16384, 2048], P(('ctx', 'tp'))
Inputs may be any that keep to these rules, and one draw needn't show every extreme that they name: beta_rate lies strictly between 0 and 1. log_decay is never positive.
All inputs are finite; a program needn't handle non-finite values.
Results may differ from a plain program's by a relative error of at most 0.014.
Values may be sent and summed in bfloat16 or wider, within the bound.
No kernel may reach another device: no remote copies, remote signals or barrier semaphores. Data moves between devices by JAX's collectives and lax.ppermute only.
A program may use at most 128 MiB of HBM per device.

v0:
```python
import jax
import jax.numpy as jnp
from jax import lax
from jax.sharding import PartitionSpec as P

HK = 16
HV = 32
DK = 128
DV = 128
BLOCK = 64


precise = lax.Precision.HIGHEST


def shifted(value, axis, steps):
    count = lax.axis_size(axis)
    initial, last = (max(0, -steps), min(count, count - steps))
    return lax.ppermute(value, axis, [(source, source + steps) for source in range(initial, last)])


def carried_in(part, axis, combine, identity):
    place = lax.axis_index(axis)
    gathered = jax.tree.map(lambda a: lax.all_gather(a, axis), part)
    state = jax.tree.map(lambda a, e: jnp.zeros_like(a) + jnp.asarray(e, a.dtype), part, identity)

    def one(lap, state):
        return combine(
            state, jax.tree.map(lambda a: lax.dynamic_index_in_dim(a, lap, 0, False), gathered)
        )

    return lax.fori_loop(0, place, one, state)


def pairwise_dot_entries(form, left, right):
    return jnp.einsum(form, left, right, precision=precise)


def causal_conv(rim_rows, raw_rows, tap_weights):
    joined = jnp.concatenate([rim_rows, raw_rows], axis=0).astype(jnp.float32)
    taps = tap_weights.astype(jnp.float32)
    row_count = raw_rows.shape[0]
    running = taps[0] * joined[0:row_count]
    for offset in range(1, tap_weights.shape[0]):
        running = running + taps[offset] * joined[offset : offset + row_count]
    return jax.nn.silu(running)


def unit_rows(key_rows):
    return key_rows * lax.rsqrt(jnp.sum(key_rows * key_rows, axis=-1, keepdims=True) + 1e-06)


def block_prep(probe_vectors, key_rows, values, strength, decay):
    block_size = decay.shape[-1]
    cumulative = jnp.cumsum(decay, axis=-1)
    row_index = lax.broadcasted_iota(jnp.int32, (block_size, block_size), 0)
    col_index = lax.broadcasted_iota(jnp.int32, (block_size, block_size), 1)
    spread = cumulative[..., :, None] - cumulative[..., None, :]
    fading = jnp.where(row_index >= col_index, jnp.exp(jnp.minimum(spread, 0.0)), 0.0)
    inner_dots = pairwise_dot_entries("...ik,...jk->...ij", key_rows, key_rows)
    lower_part = jnp.where(row_index > col_index, strength[..., :, None] * fading * inner_dots, 0.0)
    unit_lower = jnp.eye(block_size, dtype=jnp.float32) + lower_part
    cumulative_forget_ratio = jnp.exp(cumulative)
    stacked = jnp.concatenate(
        [strength[..., None] * values, (strength * cumulative_forget_ratio)[..., None] * key_rows],
        axis=-1,
    )
    solved = jax.scipy.linalg.solve_triangular(unit_lower, stacked, lower=True, unit_diagonal=True)
    value_width = values.shape[-1]
    state_updates = solved[..., :value_width]
    weight_params = solved[..., value_width:]
    causal_similarity_matrix = jnp.where(
        row_index >= col_index,
        fading * pairwise_dot_entries("...ik,...jk->...ij", probe_vectors, key_rows),
        0.0,
    )
    block_decay_factor = cumulative_forget_ratio[..., -1]
    decayed_tail_keys = jnp.exp(cumulative[..., -1:] - cumulative)[..., None] * key_rows
    return (
        probe_vectors,
        state_updates,
        weight_params,
        causal_similarity_matrix,
        cumulative_forget_ratio,
        decayed_tail_keys,
        block_decay_factor,
    )


def local_maps(arrays):
    prepared = block_prep(*arrays)
    heads = arrays[2].shape[1]
    identity_mat = jnp.broadcast_to(jnp.eye(DK, dtype=jnp.float32), (heads, DK, DK))

    def local_advance(running_recurrent_summary, block_data):
        memory_state, transition = running_recurrent_summary
        (
            probe_vectors,
            state_updates,
            weight_params,
            causal_similarity_matrix,
            cumulative_forget_ratio,
            decayed_tail_keys,
            block_decay_factor,
        ) = block_data
        residual_target_vectors = state_updates - pairwise_dot_entries(
            "ret,rtw->rew", weight_params, memory_state
        )
        emitted_vectors = cumulative_forget_ratio[..., None] * pairwise_dot_entries(
            "ret,rtw->rew", probe_vectors, memory_state
        ) + pairwise_dot_entries("keo,kov->kev", causal_similarity_matrix, residual_target_vectors)
        query_decay_map = cumulative_forget_ratio[..., None] * probe_vectors - pairwise_dot_entries(
            "hcj,hjk->hck", causal_similarity_matrix, weight_params
        )
        step_decay_map = block_decay_factor[:, None, None] * identity_mat - pairwise_dot_entries(
            "hck,hcj->hkj", decayed_tail_keys, weight_params
        )
        memory_state = block_decay_factor[:, None, None] * memory_state + pairwise_dot_entries(
            "dwn,dwm->dnm", decayed_tail_keys, residual_target_vectors
        )
        extras = (query_decay_map, step_decay_map)
        transition = pairwise_dot_entries("hkj,hjl->hkl", step_decay_map, transition)
        return ((memory_state, transition), (emitted_vectors, extras))

    zero_state = jnp.zeros((heads, DK, DV), jnp.float32)
    (memory_state, transition), (emitted_vectors, extras) = lax.scan(
        local_advance, (zero_state, identity_mat), prepared
    )
    return (emitted_vectors, extras, transition, memory_state)


def finish(pieces, starting):
    emitted_vectors, extras = (pieces[0], pieces[1])

    def finish_advance(memory_state, block_data):
        query_decay_map, step_decay_map = block_data
        return (
            pairwise_dot_entries("ufx,uxy->ufy", step_decay_map, memory_state),
            pairwise_dot_entries("ret,rtw->rew", query_decay_map, memory_state),
        )

    final_state, corrections = lax.scan(finish_advance, starting, extras)
    return emitted_vectors + corrections


def compose(earlier, later_map):
    early_trans, early_state = earlier
    late_trans, late_state = later_map
    return (
        pairwise_dot_entries("hij,hjk->hik", late_trans, early_trans),
        pairwise_dot_entries("hij,hjk->hik", late_trans, early_state) + late_state,
    )


def start_maps(heads):
    return (
        jnp.broadcast_to(jnp.eye(DK, dtype=jnp.float32), (heads, DK, DK)),
        jnp.zeros((heads, DK, DV), jnp.float32),
    )


def gate_norm(core_out, gate_values, norm_gain):
    gate_part = gate_values.astype(jnp.float32).reshape(core_out.shape)
    scaling = lax.rsqrt(jnp.mean(core_out * core_out, axis=-1, keepdims=True) + 1e-06)
    gated = (core_out * scaling * norm_gain * jax.nn.silu(gate_part)).astype(jnp.bfloat16)
    return gated.reshape(core_out.shape[0], core_out.shape[1] * core_out.shape[2])


def local(
    query_in,
    key_in,
    value_in,
    gate_values,
    query_conv,
    key_conv,
    value_conv,
    beta_rate,
    log_decay,
    norm_gain,
    out_weight,
):
    head_ratio = HV // HK
    taps_count = query_conv.shape[0]
    row_count = query_in.shape[0]
    block_count = row_count // BLOCK
    query_cols = query_in.shape[1]
    key_cols = key_in.shape[1]
    tail_rows = jnp.concatenate(
        [
            query_in[row_count - taps_count + 1 :],
            key_in[row_count - taps_count + 1 :],
            value_in[row_count - taps_count + 1 :],
        ],
        axis=1,
    )
    rim_rows = shifted(tail_rows, "ctx", 1)
    probe_vectors = causal_conv(rim_rows[:, :query_cols], query_in, query_conv)
    key_rows = causal_conv(rim_rows[:, query_cols : query_cols + key_cols], key_in, key_conv)
    values = causal_conv(rim_rows[:, query_cols + key_cols :], value_in, value_conv)
    key_heads = query_cols // DK
    value_heads = value_in.shape[1] // DV
    probe_vectors = jnp.repeat(
        probe_vectors.reshape(block_count, BLOCK, key_heads, DK).transpose(0, 2, 1, 3),
        head_ratio,
        axis=1,
    )
    key_rows = jnp.repeat(
        unit_rows(key_rows.reshape(block_count, BLOCK, key_heads, DK)).transpose(0, 2, 1, 3),
        head_ratio,
        axis=1,
    )
    values = values.reshape(block_count, BLOCK, value_heads, DV).transpose(0, 2, 1, 3)
    strength = beta_rate.reshape(value_heads, block_count, BLOCK).transpose(1, 0, 2)
    decay = log_decay.reshape(value_heads, block_count, BLOCK).transpose(1, 0, 2)
    arrays = (probe_vectors, key_rows, values, strength, decay)
    all_heads = local_maps(arrays)
    prefix = carried_in((all_heads[2], all_heads[3]), "ctx", compose, start_maps(value_heads))
    core_out = finish(all_heads, prefix[1])
    core_out = core_out.transpose(0, 2, 1, 3).reshape(row_count, value_heads, DV)
    gated = gate_norm(core_out, gate_values, norm_gain)
    return lax.psum_scatter(
        jnp.dot(gated, out_weight, preferred_element_type=jnp.float32).astype(jnp.bfloat16),
        "tp",
        scatter_dimension=0,
        tiled=True,
    )


def solution(mesh):
    return jax.shard_map(
        local,
        mesh=mesh,
        in_specs=(
            P("ctx", "tp"),
            P("ctx", "tp"),
            P("ctx", "tp"),
            P("ctx", "tp"),
            P(None, "tp"),
            P(None, "tp"),
            P(None, "tp"),
            P("tp", "ctx"),
            P("tp", "ctx"),
            P(),
            P("tp", None),
        ),
        out_specs=P(("ctx", "tp"), None),
        check_vma=False,
    )
```

profile of v0, /device:TPU:1, one launch (start us, length us, event | category | flops | bytes accessed | tf_op | source)
XLA Modules:
  0.0 600.0 jit_solution(1486982784773749315)
XLA Ops:
  8.8 4.0 collective-permute-start
  19.1 1.4 fusion.89
  23.5 2.7 fusion.56
  26.2 80.0 %custom-call.4 = f32[4,4,1,64,64]{3,4,2,1,0:T(8,128)} custom-call(f32[4,4,1,64,64]{4,3,2,1,0:T(8,128)} %fusion.56), custom_call_target="InvertDiagBlocksLowerTriangular" | custom-call | tf_op jit(solution)/shard_map/jit(_solve_triangular)/vmap(vmap())/triangular_solve | solution.py:68
  108.4 2.0 reshape.83
  112.8 2.1 fusion.57
  118.6 3.0 fusion.51
  123.3 44.4 %while.45 = (s32[]{:T(128)}, f32[4,128,128]{2,1,0:T(8,128)S(1)}, f32[4,128,128]{2,1,0:T(8,128)S(1)}, f32[4,4,64,128]{3,2,1,0:T(8,128)}, f32[4,4,64,128]{3,2,1,0:...) while((s32[]{:T(128)}, f32[4,128,128]{2,1,0:T(8,128)S(1)}, ...), condition=%wide.region_3.4_spmd.clone, body=%wide.region_2.3_spmd.clone.sunk | while | flops 352944128 | bytes 5189337 | solution.py:126
  125.8 1.9 fusion.154
  128.4 1.5 convolution_add_fusion.5
  129.9 2.2 bitcast_dynamic-update-slice_fusion.2
  132.5 1.9 fusion.155
  136.9 1.9 fusion.154
  139.5 1.5 convolution_add_fusion.5
  141.0 2.2 bitcast_dynamic-update-slice_fusion.2
  143.6 1.9 fusion.155
  148.0 1.9 fusion.154
  150.6 1.5 convolution_add_fusion.5
  152.1 2.2 bitcast_dynamic-update-slice_fusion.2
  154.7 1.9 fusion.155
  159.1 1.9 fusion.154
  161.7 1.5 convolution_add_fusion.5
  163.2 2.2 bitcast_dynamic-update-slice_fusion.2
  165.8 1.9 fusion.155
  169.3 142.9 %all-gather.5.cloned.1.call-done = f32[256,128,128]{2,1,0:T(8,128)} async-done(((f32[4,128,128]{2,1,0:T(8,128)}), f32[256,128,128]{2,1,0:T(8,128)}) %all-gather.5.cloned.1.call-update) | async-done | bytes 16777232 | tf_op jit(solution)/shard_map/all_gather | solution.py:24
  312.2 140.9 %all-gather.7.cloned.1.call-done = f32[256,128,128]{2,1,0:T(8,128)} async-done(((f32[4,128,128]{2,1,0:T(8,128)}), f32[256,128,128]{2,1,0:T(8,128)}) %all-gather.7.cloned.1.call-update) | async-done | bytes 16777232 | tf_op jit(solution)/shard_map/all_gather | solution.py:24
  453.2 10.7 %while.44 = (s32[]{:T(128)}, f32[4,128,128]{2,1,0:T(8,128)S(1)}, f32[4,4,64,128]{3,2,1,0:T(8,128)S(1)}, f32[4,4,128,128]{3,2,1,0:T(8,128)}, f32[4,4,64,128]{3,2,1,0:T(8,128)}, /*index=5*/s32[]{:T(128)}) while((s32[]{:T(128)}, f32[4,128,128]{2,1,0:T(8,128)S(1)}, f32[4,4,64,128]{3,2,1,0:T(8,128)S(1)}, f32[4,4,128,128]{3,2,1,0:T(8,128)}, ...), condition=%wide.region_7.8_spmd, body=%wide.region_6.7_spmd.sunk | while | flops 150994944 | bytes 1836613 | solution.py:142
  457.2 1.3 fusion.136
  459.9 1.3 fusion.136
  464.9 1.4 copy.36
  466.7 2.7 convolution_convert_fusion
  469.4 124.1 %reduce-scatter.2.cloned.1.call-done = bf16[32,2048]{1,0:T(8,128)(2,1)} async-done(((bf16[256,2048]{1,0:T(8,128)(2,1)}), bf16[32,2048]{1,0:T(8,128)(2,1)}) %reduce-scatter.2.cloned.1.call-update) | async-done | bytes 131088 | tf_op jit(solution)/shard_map/reduce_scatter | solution.py:221
  (106 shorter events, 46.3 us)
Async XLA Ops:
  6.5 460.1 %copy-start = (bf16[512,2048]{1,0:T(8,128)(2,1)S(1)}, bf16[512,2048]{1,0:T(8,128)(2,1)}, u32[]{:S(2)}) copy-start(bf16[512,2048]{1,0:T(8,128)(2,1)} %param.27) | copy-start | bytes 6291460
  6.5 305.7 %all-gather.5.cloned.1.call-start = ((), (), s32[]{:S(2)}) async-start(), calls=%async_computation.2 | async-start | bytes 17039360 | tf_op jit(solution)/shard_map/all_gather | solution.py:24
  8.8 12.6 %collective-permute-start = (bf16[3,1024]{1,0:T(4,128)(2,1)S(1)}, bf16[3,1024]{1,0:T(4,128)(2,1)S(1)}, u32[]{:S(2)}, u32[]{:S(2)}) collective-permute-start(bf16[3,1024]{1,0:T(4,128)(2,1)S(1)} %pad_maximum_fusion), channel_id=1, source_target_pairs={{0,8},{8,16},{16,24},{24,32},{32,40},{40,48},{48,56},{56,64},{64,7... | collective-permute-start | bytes 18440 | tf_op jit(solution)/shard_map/ppermute | solution.py:19
  23.5 89.3 %copy-start.4 = (f32[4,2,2,64,128]{4,3,2,1,0:T(8,128)}, f32[4,2,2,64,128]{4,3,2,1,0:T(8,128)S(1)}, u32[]{:S(2)}) copy-start(f32[4,2,2,64,128]{4,3,2,1,0:T(8,128)S(1)} %broadcast_in_dim.59) | copy-start | bytes 1572868
  115.8 53.4 %copy-start.6 = (f32[128]{0:T(128)S(1)}, f32[128]{0:T(128)}, u32[]{:S(2)}) copy-start(f32[128]{0:T(128)} %param.26) | copy-start | bytes 1540
  118.6 4.7 copy-start.3
  167.7 0.7 copy-start.2
  167.7 0.8 copy-start.1
  167.7 296.2 %copy-start.5 = (f32[4,4,64,128]{3,2,1,0:T(8,128)S(1)}, f32[4,4,64,128]{3,2,1,0:T(8,128)}, u32[]{:S(2)}) copy-start(f32[4,4,64,128]{3,2,1,0:T(8,128)} %get-tuple-element.152) | copy-start | bytes 1572868
  168.4 284.7 %all-gather.7.cloned.1.call-start = ((), (), s32[]{:S(2)}) async-start(), calls=%async_computation.3 | async-start | bytes 17039360 | tf_op jit(solution)/shard_map/all_gather | solution.py:24
  169.2 424.3 %reduce-scatter.2.cloned.1.call-start = ((), (), s32[]{:S(2)}) async-start(), calls=%async_computation.1 | async-start | bytes 1179648 | tf_op jit(solution)/shard_map/reduce_scatter | solution.py:221
Sparse Core Ops, SparseCore 0:
  168.6 143.5 all-gather.4
  315.3 137.8 all-gather.6
  469.5 123.8 reduce-scatter.1
where the time goes:
time: 603 us; the launch traced here: 600 us
  waiting for transfers between devices  409 us (68%)
  other arithmetic  91.1 us (15%)
  matrix products  62.3 us (10%)
  local copies, waits for them, and re-layouts  20.2 us (3%)
  between operations  13.3 us (2%)
    all_gather x2, waiting for transfers between devices, carried_in(): gathered = jax.tree.map(lambda a: lax.all_gather(a, axis), part)  284 us
    reduce_scatter x1, waiting for transfers between devices, local(): lax.psum_scatter(jnp.dot(gated, out_weight, preferred_element_type=jnp.fl...  124 us
    another operation x4, other arithmetic, block_prep(): jax.scipy.linalg.solve_triangular(unit_lower, stacked, lower=True, unit_d...  81.3 us
    dot_general x38, matrix products, pairwise_dot_entries(): return jnp.einsum(form, left, right, precision=precise)  57.5 us
  transfers between devices with their start and end apart: 4, of which 3 were waited for; matrix products, arithmetic and copies ran while one was open for 1% of the time, Pallas kernels for 0%

commit v1 on v0

v1 whole, which is shorter than its diff:
```python
import functools

import jax
import jax.numpy as jnp
from jax import lax
from jax.experimental import pallas as pl
from jax.experimental.pallas import tpu as pltpu
from jax.sharding import Mesh
from jax.sharding import PartitionSpec as P

DK = 128
DV = 128
F32 = jnp.float32
BF16 = jnp.bfloat16
INTERPRET = False

NN = (((1,), (0,)), ((), ()))
NT = (((1,), (1,)), ((), ()))
TN = (((0,), (0,)), ((), ()))


def dot(a, b, dims=NN):
    return lax.dot_general(a, b, dims, preferred_element_type=F32)


def split(x):
    high = x.astype(BF16)
    return high, (x - high.astype(F32)).astype(BF16)


def dot3(a, b, dims=NN):
    return dot(a[0], b[0], dims) + (dot(a[0], b[1], dims) + dot(a[1], b[0], dims))


def dot2(a, b, dims=NN):
    return dot(a[0], b, dims) + dot(a[1], b, dims)


def silu(x):
    return x / (1.0 + jnp.exp(-x))


def conv(rim, raw, taps):
    joined = jnp.concatenate([rim, raw], axis=0).astype(F32)
    taps = taps.astype(F32)
    rows = raw.shape[0]
    count = taps.shape[0]
    base = rim.shape[0] - (count - 1)
    running = taps[0:1] * joined[base : base + rows]
    for offset in range(1, count):
        running = running + taps[offset : offset + 1] * joined[base + offset : base + offset + rows]
    return silu(running)


def prepare_kernel(
    rim_ref, q_ref, k_ref, v_ref, qt_ref, kt_ref, vt_ref, beta_ref, decay_ref, maps_ref, base_ref, reach_ref
):
    rows = q_ref.shape[0]
    heads = beta_ref.shape[0]
    key_heads = q_ref.shape[1] // DK
    ratio = heads // key_heads
    q_cols = q_ref.shape[1]

    row = lax.broadcasted_iota(jnp.int32, (rows, rows), 0)
    col = lax.broadcasted_iota(jnp.int32, (rows, rows), 1)
    lower = row >= col
    strict = row > col
    ones = jnp.where(lower, 1.0, 0.0).astype(BF16)
    eye = jnp.where(row == col, 1.0, 0.0)
    eye_b = eye.astype(BF16)

    both = jnp.concatenate([decay_ref[...], beta_ref[...]], axis=0)
    high = both.astype(BF16)
    rest = both - high.astype(F32)
    mid = rest.astype(BF16)
    low = (rest - mid.astype(F32)).astype(BF16)
    upto_col = dot(ones, high, NT) + (dot(ones, mid, NT) + dot(ones, low, NT))
    upto_row = dot(high, ones, NT) + (dot(mid, ones, NT) + dot(low, ones, NT))
    plain_col = dot(eye_b, high, NT) + (dot(eye_b, mid, NT) + dot(eye_b, low, NT))

    keys = []
    inner = []
    cross = []
    queries = []
    for g in range(key_heads):
        cols = slice(g * DK, (g + 1) * DK)
        q = conv(rim_ref[:, cols], q_ref[:, cols], qt_ref[:, cols])
        k = conv(rim_ref[:, q_cols + g * DK : q_cols + (g + 1) * DK], k_ref[:, cols], kt_ref[:, cols])
        k = k * lax.rsqrt(jnp.sum(k * k, axis=-1, keepdims=True) + 1e-06)
        k_parts = split(k)
        queries.append(q)
        keys.append(k)
        inner.append(dot3(k_parts, k_parts, NT))
        cross.append(dot3(split(q), k_parts, NT))

    lowers = []
    solved = []
    sims = []
    for h in range(heads):
        g = h // ratio
        fading = jnp.where(lower, jnp.exp(jnp.minimum(upto_col[:, h : h + 1] - upto_row[h : h + 1, :], 0.0)), 0.0)
        beta = plain_col[:, heads + h : heads + h + 1]
        lower_part = jnp.where(strict, beta * fading * inner[g], 0.0)
        sims.append(split(fading * cross[g]))
        lowers.append(split(lower_part))
        solved.append(eye - jnp.where((row // 2 == col // 2), lower_part, 0.0))

    size = 2
    while size < rows:
        pick = (row // (2 * size) == col // (2 * size)) & (row // size > col // size)
        for h in range(heads):
            off = tuple(jnp.where(pick, part, jnp.zeros_like(part)) for part in lowers[h])
            x = split(solved[h])
            solved[h] = solved[h] - dot3(x, split(dot3(off, x)))
        size *= 2

    for h in range(heads):
        g = h // ratio
        vcols = slice(h * DV, (h + 1) * DV)
        start = q_cols * 2 + h * DV
        v = conv(rim_ref[:, start : start + DV], v_ref[:, vcols], vt_ref[:, vcols])
        beta = plain_col[:, heads + h : heads + h + 1]
        reach = jnp.exp(upto_col[:, h : h + 1])
        last = upto_col[rows - 1 : rows, h : h + 1]
        right = jnp.concatenate([(beta * reach) * keys[g], beta * v], axis=1)
        answer = split(dot3(split(solved[h]), split(right)))
        tail = jnp.exp(last - upto_col[:, h : h + 1]) * keys[g]
        folded = dot3(answer, split(tail), TN)
        emitted = dot3(sims[h], answer)
        base_ref[:, vcols] = emitted[:, DK:]
        reach_ref[:, vcols] = (reach * queries[g] - emitted[:, :DK]).astype(BF16)
        square = jnp.where(row[:DK, :DK] == col[:DK, :DK], jnp.exp(last), 0.0)
        step_map = (square - folded[:DK]).astype(BF16)
        added = folded[DK:].astype(BF16)
        half = DV // 2
        maps_ref[2 * h, :DK] = step_map
        maps_ref[2 * h + 1, :DK] = step_map
        maps_ref[2 * h, DK:] = added[:half]
        maps_ref[2 * h + 1, DK:] = added[half:]


def line_kernel(maps_ref, prefix_ref, total_ref):
    count = maps_ref.shape[0]
    rows = maps_ref.shape[1]
    row = lax.broadcasted_iota(jnp.int32, (rows, DK), 0)
    col = lax.broadcasted_iota(jnp.int32, (rows, DK), 1)
    prefix_ref[0] = jnp.where(row == col, 1.0, 0.0)
    running = maps_ref[0].astype(F32)
    for place in range(1, count):
        prefix_ref[place] = running
        added = jnp.where(row >= DK, maps_ref[place].astype(F32), 0.0)
        running = dot2(split(running), maps_ref[place, :DK]) + added
    total = running.astype(BF16)
    for place in range(total_ref.shape[0]):
        total_ref[place] = total


def start_kernel(place_ref, totals_ref, prefix_ref, state_ref):
    count = totals_ref.shape[0]
    place = place_ref[0]
    half = totals_ref.shape[1] - DK
    state = jnp.zeros((half, DK), F32)
    for earlier in range(count - 1):
        later = totals_ref[earlier, DK:].astype(F32)
        if earlier > 0:
            later = later + dot2(split(state), totals_ref[earlier, :DK])
        state = jnp.where(earlier < place, later, state)
    parts = split(state)
    for step in range(prefix_ref.shape[0]):
        moved = prefix_ref[step, DK:] + dot3(parts, split(prefix_ref[step, :DK]))
        state_ref[step] = moved.astype(BF16)


def finish_kernel(base_ref, reach_ref, state_ref, gate_ref, gain_ref, weight_ref, out_ref):
    heads = base_ref.shape[1] // DV
    gain = gain_ref[...]
    pieces = []
    for h in range(heads):
        cols = slice(h * DV, (h + 1) * DV)
        core = base_ref[:, cols] + dot(reach_ref[:, cols], state_ref[h], NT)
        scale = lax.rsqrt(jnp.mean(core * core, axis=-1, keepdims=True) + 1e-06)
        gate = silu(gate_ref[:, cols].astype(F32))
        pieces.append((core * scale * gain * gate).astype(BF16))
    gated = jnp.concatenate(pieces, axis=1)
    width = 512
    for start in range(0, out_ref.shape[1], width):
        cols = slice(start, start + width)
        out_ref[:, cols] = dot(gated, weight_ref[:, cols]).astype(BF16)


def call(kernel, outs, *args, scalars=0):
    vmem = pl.BlockSpec(memory_space=pltpu.VMEM)
    smem = pl.BlockSpec(memory_space=pltpu.SMEM)
    return pl.pallas_call(
        kernel,
        out_shape=outs,
        in_specs=[smem] * scalars + [vmem] * (len(args) - scalars),
        out_specs=jax.tree.map(lambda _: vmem, outs),
        compiler_params=pltpu.CompilerParams(vmem_limit_bytes=48 << 20),
        interpret=INTERPRET,
    )(*args)


def local(
    nz,
    ny,
    ntp,
    query_in,
    key_in,
    value_in,
    gate_values,
    query_conv,
    key_conv,
    value_conv,
    beta_rate,
    log_decay,
    norm_gain,
    out_weight,
):
    shape = jax.ShapeDtypeStruct
    rows = query_in.shape[0]
    heads = beta_rate.shape[0]
    rim = 16
    tail_rows = jnp.concatenate([a[rows - rim :] for a in (query_in, key_in, value_in)], axis=1)
    count = nz * ny
    rim_rows = lax.ppermute(tail_rows, ("z", "y"), [(i, i + 1) for i in range(count - 1)])

    half = DV // 2
    maps, base, reach = call(
        prepare_kernel,
        (
            shape((2 * heads, DK + half, DK), BF16),
            shape((rows, heads * DV), F32),
            shape((rows, heads * DK), BF16),
        ),
        rim_rows, query_in, key_in, value_in, query_conv, key_conv, value_conv, beta_rate, log_decay,
    )
    maps = lax.all_to_all(maps, "y", 0, 0, tiled=True)
    prefix, totals = call(
        line_kernel, (shape((ny, DK + half, DK), F32), shape((nz, DK + half, DK), BF16)), maps
    )
    totals = lax.all_to_all(totals, "z", 0, 0, tiled=True)
    place = lax.axis_index("z").reshape(1).astype(jnp.int32)
    states = call(start_kernel, shape((ny, half, DK), BF16), place, totals, prefix, scalars=1)
    states = lax.all_to_all(states, "y", 0, 0, tiled=True)
    partial = call(
        finish_kernel,
        shape((rows, out_weight.shape[1]), BF16),
        base, reach, states.reshape(heads, DV, DK), gate_values, norm_gain.reshape(1, DV), out_weight,
    )
    parts = lax.all_to_all(partial.reshape(ntp, rows // ntp, -1), "tp", 0, 0, tiled=True)
    return jnp.sum(parts.astype(F32), axis=0).astype(BF16)


def build(mesh):
    nz, ny, ntp = mesh.devices.shape
    ctx = ("z", "y")
    return jax.shard_map(
        functools.partial(local, nz, ny, ntp),
        mesh=mesh,
        in_specs=(
            P(ctx, "tp"),
            P(ctx, "tp"),
            P(ctx, "tp"),
            P(ctx, "tp"),
            P(None, "tp"),
            P(None, "tp"),
            P(None, "tp"),
            P("tp", ctx),
            P("tp", ctx),
            P(),
            P("tp", None),
        ),
        out_specs=P((*ctx, "tp"), None),
        check_vma=False,
    )


def solution(mesh):
    return build(Mesh(mesh.devices.reshape(8, 8, 8), ("z", "y", "tp")))
```

time: 603 us -> 109 us (0.18)
  waiting for transfers between devices: 409 us -> 11.8 us
  other arithmetic: 91.1 us -> 0.82 us
  matrix products: 62.3 us -> 0 us
  blocking collectives: 0 us -> 57 us
  between operations: 13.3 us -> 0.08 us
  Pallas kernels: 0 us -> 12.8 us
  starting transfers between devices: 4.1 us -> 14.2 us
  local copies, waits for them, and re-layouts: 20.2 us -> 11.8 us
    all_gather x2 -> x0, waiting for transfers between devices: 284 us -> none  [carried_in(): gathered = jax.tree.map(lambda a: lax.all_gather(a, axis), part)]
    reduce_scatter x1 -> x0, waiting for transfers between devices: 124 us -> none  [local(): lax.psum_scatter(jnp.dot(gated, out_weight, preferred_element_type=jnp.fl...]
    another operation x5 -> x0, other arithmetic: 82.3 us -> none  [the longest x4 81.3 us: block_prep(): jax.scipy.linalg.solve_triangular(unit_lower, stacked, lower=True, unit_d...]
    dot_general x39 -> x0, matrix products: 60.2 us -> none  [the longest x38 57.5 us: pairwise_dot_entries(): return jnp.einsum(form, left, right, precision=precise)]
    all_to_all x0 -> x3, blocking collectives: none -> 57 us  [the longest x1 23.1 us: local(): lax.all_to_all(partial.reshape(ntp, rows // ntp, -1), 'tp', 0, 0, tiled=T...]
    pallas_call x0 -> x4, Pallas kernels: none -> 12.8 us  [call(): pl.pallas_call(kernel, out_shape=outs, in_specs=[smem] * scalars + [vmem]...]
    all_to_all x0 -> x1, waiting for transfers between devices: none -> 10.8 us  [local(): totals = lax.all_to_all(totals, 'z', 0, 0, tiled=True)]
    all_to_all x0 -> x1, starting transfers between devices: none -> 10 us  [local(): totals = lax.all_to_all(totals, 'z', 0, 0, tiled=True)]
  transfers between devices with their start and end apart: 4 -> 2, of which waited for: 3 -> 2; matrix products, arithmetic and copies ran while one was open for 1% -> 0% of each run, Pallas kernels for 0% -> 0%
where the time goes in v1:
time: 109 us
  blocking collectives  57 us (52%)
  starting transfers between devices  14.2 us (13%)
  Pallas kernels  12.8 us (12%)
  local copies, waits for them, and re-layouts  11.8 us (11%)
  waiting for transfers between devices  11.8 us (11%)
    all_to_all x1, blocking collectives, local(): lax.all_to_all(partial.reshape(ntp, rows // ntp, -1), 'tp', 0, 0, tiled=T...  23.1 us
    all_to_all x1, blocking collectives, local(): maps = lax.all_to_all(maps, 'y', 0, 0, tiled=True)  20 us
    all_to_all x1, blocking collectives, local(): states = lax.all_to_all(states, 'y', 0, 0, tiled=True)  13.9 us
    pallas_call x4, Pallas kernels, call(): pl.pallas_call(kernel, out_shape=outs, in_specs=[smem] * scalars + [vmem]...  12.8 us
    all_to_all x1, waiting for transfers between devices, local(): totals = lax.all_to_all(totals, 'z', 0, 0, tiled=True)  10.8 us
    all_to_all x1, starting transfers between devices, local(): totals = lax.all_to_all(totals, 'z', 0, 0, tiled=True)  10 us
    unnamed x32, local copies, waits for them, and re-layouts  9.71 us
    ppermute x1, starting transfers between devices, local(): lax.ppermute(tail_rows, ('z', 'y'), [(i, i + 1) for i in range(count - 1)])  4.14 us
  transfers between devices with their start and end apart: 2, of which 2 were waited for; matrix products, arithmetic and copies ran while one was open for 0% of the time, Pallas kernels for 0%

profile of v1, /device:TPU:1, one launch (start us, length us, event | category | flops | bytes accessed | tf_op | source)
XLA Modules:
  0.0 108.5 jit_solution(15046971267499664337)
XLA Ops:
  0.0 0.7 slice.11
  0.7 0.7 slice.10
  1.4 0.7 slice.9
  2.1 4.1 %collective-permute-start = (bf16[16,1024]{1,0:T(8,128)(2,1)S(1)}, bf16[16,1024]{1,0:T(8,128)(2,1)S(1)}, u32[]{:S(2)}, u32[]{:S(2)}) collective-permute-start(bf16[16,1024]{1,0:T(8,128)(2,1)S(1)} %pad_maximum_fusion), channel_id=1, source_target_pairs={{0,8},{8,16},{16,24},{24,32},{32,40},{40,48},{48,56},{56,64},{64,7... | collective-permute-start | bytes 98312 | tf_op jit(solution)/shard_map/ppermute | solution.py:226
  6.3 1.0 collective-permute-done.rim_ref
  7.3 0.9 copy-done.4
  8.2 0.9 copy-done.8
  9.1 0.9 copy-done.9
  10.1 0.7 copy-done.10
  10.7 0.7 copy-done.11
  11.4 0.7 copy-done.12
  12.1 0.7 copy-done.13
  12.8 0.7 copy-done.14
  13.5 9.5 %shard_map.109 = (bf16[8,192,128]{2,1,0:T(8,128)(2,1)S(1)}, f32[256,512]{1,0:T(8,128)S(1)}, bf16[256,512]{1,0:T(8,128)(2,1)S(1)}) custom-call(bf16[16,1024]{1,0:T(8,128)(2,1)S(1)} %collective-permute-done.rim_ref, bf16[256,256]{1,0:T(8,128)(2,1)S(1)} %copy-done.9, bf16[256,256]{1,0:T(8,128)(2,1)S(1)} %copy-done.8, bf16[256,512]{1,0:T(8,128)(2,1)S(1)} %copy-done.4, ...), custom_call_target="tpu_custom_call" | custom-call | tf_op jit(solution)/shard_map/pallas_call | solution.py:194
  23.0 0.0 copy-start.1
  23.0 0.8 copy-done.1
  23.8 20.0 %all_to_all.20.maps_ref = bf16[8,192,128]{2,1,0:T(8,128)(2,1)S(1)} all-to-all(bf16[8,192,128]{2,1,0:T(8,128)(2,1)S(1)} %get-tuple-element.12), channel_id=1, replica_groups=mesh['z'=8,'y'=8,'tp'=8] {'y'}, dimensions={0} | all-to-all | bytes 786432 | tf_op jit(solution)/shard_map/all_to_all | solution.py:238
  43.8 1.1 shard_map.110
  44.9 0.0 copy-done.6
  44.9 0.0 copy-start.3
  44.9 0.7 copy-done.3
  45.6 10.0 %all-to-all-start.1 = ((bf16[8,192,128]{2,1,0:T(8,128)(2,1)}), bf16[8,192,128]{2,1,0:T(8,128)(2,1)S(1)}, u32[]{:S(2)}, u32[]{:S(2)}) async-start(bf16[8,192,128]{2,1,0:T(8,128)(2,1)} %copy-done.3), calls=%async_computation.1 | async-start | bytes 786432 | tf_op jit(solution)/shard_map/all_to_all | solution.py:242
  55.7 10.8 %all-to-all-done.1.totals_ref = bf16[8,192,128]{2,1,0:T(8,128)(2,1)S(1)} async-done(((bf16[8,192,128]{2,1,0:T(8,128)(2,1)}), bf16[8,192,128]{2,1,0:T(8,128)(2,1)S(1)}, u32[]{:S(2)}, u32[]{:S(2)}) %all-to-all-start.1) | async-done | bytes 393248 | tf_op jit(solution)/shard_map/all_to_all | solution.py:242
  66.4 1.2 %shard_map.111 = bf16[8,64,128]{2,1,0:T(8,128)(2,1)S(1)} custom-call(s32[1]{0:T(128)} %bitcast.place_ref, bf16[8,192,128]{2,1,0:T(8,128)(2,1)S(1)} %all-to-all-done.1.totals_ref, f32[8,192,128]{2,1,0:T(8,128)S(1)} %get-tuple-element.14.prefix_ref), custom_call_target="tpu_custom_call" | custom-call | tf_op jit(solution)/shard_map/pallas_call | solution.py:194
  67.6 13.9 %all_to_all.21 = bf16[8,64,128]{2,1,0:T(8,128)(2,1)S(1)} all-to-all(bf16[8,64,128]{2,1,0:T(8,128)(2,1)S(1)} %shard_map.111), channel_id=1, replica_groups=mesh['z'=8,'y'=8,'tp'=8] {'y'}, dimensions={0} | all-to-all | bytes 262144 | tf_op jit(solution)/shard_map/all_to_all | solution.py:245
  81.5 0.0 copy-done.15
  81.5 0.0 copy-done
  81.6 1.0 copy-done.2
  82.6 0.9 copy-done.7
  83.5 1.0 shard_map.112
  84.6 23.1 %all_to_all.22 = bf16[8,32,2048]{2,1,0:T(8,128)(2,1)S(1)} all-to-all(bf16[8,32,2048]{2,1,0:T(8,128)(2,1)S(1)} %bitcast.4), channel_id=1, replica_groups=mesh['z'=8,'y'=8,'tp'=8] {'tp'}, dimensions={0} | all-to-all | bytes 2097152 | tf_op jit(solution)/shard_map/all_to_all | solution.py:251
  107.7 0.8 reduce_sum.12
  (16 shorter events, 0.0 us)
Async XLA Ops:
  1.4 80.1 %copy-start.15 = (f32[128]{0:T(128)S(1)}, f32[128]{0:T(128)}, u32[]{:S(2)}) copy-start(f32[128]{0:T(128)} %param.20) | copy-start | bytes 1540
  2.1 79.4 %copy-start = (bf16[512,2048]{1,0:T(8,128)(2,1)S(1)}, bf16[512,2048]{1,0:T(8,128)(2,1)}, u32[]{:S(2)}) copy-start(bf16[512,2048]{1,0:T(8,128)(2,1)} %weight_ref.1) | copy-start | bytes 6291460
  2.1 5.2 %collective-permute-start = (bf16[16,1024]{1,0:T(8,128)(2,1)S(1)}, bf16[16,1024]{1,0:T(8,128)(2,1)S(1)}, u32[]{:S(2)}, u32[]{:S(2)}) collective-permute-start(bf16[16,1024]{1,0:T(8,128)(2,1)S(1)} %pad_maximum_fusion), channel_id=1, source_target_pairs={{0,8},{8,16},{16,24},{24,32},{32,40},{40,48},{48,56},{56,64},{64,7... | collective-permute-start | bytes 98312 | tf_op jit(solution)/shard_map/ppermute | solution.py:226
  7.3 0.9 copy-start.4
  8.2 0.9 copy-start.8
  9.1 0.9 copy-start.9
  10.1 0.7 copy-start.10
  10.7 0.7 copy-start.11
  11.4 0.7 copy-start.12
  12.1 0.7 copy-start.13
  12.8 0.7 copy-start.14
  13.5 68.1 %copy-start.5 = (bf16[256,512]{1,0:T(8,128)(2,1)S(1)}, bf16[256,512]{1,0:T(8,128)(2,1)}, u32[]{:S(2)}) copy-start(bf16[256,512]{1,0:T(8,128)(2,1)} %gate_ref.1) | copy-start | bytes 786436
  23.0 0.8 copy-start.1
  23.8 21.0 %copy-start.6 = (bf16[256,512]{1,0:T(8,128)(2,1)}, bf16[256,512]{1,0:T(8,128)(2,1)S(1)}, u32[]{:S(2)}) copy-start(bf16[256,512]{1,0:T(8,128)(2,1)S(1)} %get-tuple-element.11.reach_ref) | copy-start | bytes 786436
  44.9 0.7 copy-start.3
  45.6 20.8 %all-to-all-start.1 = ((bf16[8,192,128]{2,1,0:T(8,128)(2,1)}), bf16[8,192,128]{2,1,0:T(8,128)(2,1)S(1)}, u32[]{:S(2)}, u32[]{:S(2)}) async-start(bf16[8,192,128]{2,1,0:T(8,128)(2,1)} %copy-done.3), calls=%async_computation.1 | async-start | bytes 786432 | tf_op jit(solution)/shard_map/all_to_all | solution.py:242
  81.6 1.0 copy-start.2
  82.6 0.9 copy-start.7

commit v2 on v1

v2 whole, which is shorter than its diff:
```python
import functools

import jax
import jax.numpy as jnp
from jax import lax
from jax.experimental import pallas as pl
from jax.experimental.pallas import tpu as pltpu
from jax.sharding import Mesh
from jax.sharding import PartitionSpec as P

DK = 128
DV = 128
F32 = jnp.float32
BF16 = jnp.bfloat16
INTERPRET = False
REACH_LIMIT = 60

NN = (((1,), (0,)), ((), ()))
NT = (((1,), (1,)), ((), ()))
TN = (((0,), (0,)), ((), ()))


def dot(a, b, dims=NN):
    return lax.dot_general(a, b, dims, preferred_element_type=F32)


def split(x):
    high = x.astype(BF16)
    return high, (x - high.astype(F32)).astype(BF16)


def dot3(a, b, dims=NN):
    return dot(a[0], b[0], dims) + (dot(a[0], b[1], dims) + dot(a[1], b[0], dims))


def dot2(a, b, dims=NN):
    return dot(a[0], b, dims) + dot(a[1], b, dims)


def silu(x):
    return x / (1.0 + jnp.exp(-x))


def conv(rim, raw, taps):
    joined = jnp.concatenate([rim, raw], axis=0).astype(F32)
    taps = taps.astype(F32)
    rows = raw.shape[0]
    count = taps.shape[0]
    base = rim.shape[0] - (count - 1)
    running = taps[0:1] * joined[base : base + rows]
    for offset in range(1, count):
        running = running + taps[offset : offset + 1] * joined[base + offset : base + offset + rows]
    return silu(running)


def fetch(pairs, sems):
    copies = [pltpu.make_async_copy(src, dst, sems.at[i]) for i, (src, dst) in enumerate(pairs)]
    for copy in copies:
        copy.start()
    return copies


def tail_kernel(q_hbm, k_hbm, v_hbm, out_ref, sems):
    rows = q_hbm.shape[0]
    count = out_ref.shape[0]
    start = 0
    pairs = []
    for source in (q_hbm, k_hbm, v_hbm):
        width = source.shape[1]
        pairs.append((source.at[pl.ds(rows - count, count)], out_ref.at[:, pl.ds(start, width)]))
        start += width
    for copy in fetch(pairs, sems):
        copy.wait()


def wide_left(parts):
    return jnp.concatenate(parts, axis=1)


def wide_right(parts):
    high, low = parts
    top = jnp.concatenate([high, low], axis=1)
    return jnp.concatenate([top, jnp.concatenate([high, jnp.zeros_like(low)], axis=1)], axis=0)


def packed(left, right):
    both = dot(left, right)
    width = both.shape[1] // 2
    return both[:, :width] + both[:, width:]


def triangle(shape):
    row = lax.broadcasted_iota(jnp.int32, shape, 0)
    col = lax.broadcasted_iota(jnp.int32, shape, 1)
    return row, col


def exact_sums(left, value, dims, swap):
    high = value.astype(BF16)
    rest = value - high.astype(F32)
    mid = rest.astype(BF16)
    low = (rest - mid.astype(F32)).astype(BF16)
    parts = [dot(p, left, dims) if swap else dot(left, p, dims) for p in (high, mid, low)]
    return parts[0] + (parts[1] + parts[2])


def prepare_kernel(
    rim_hbm,
    k_hbm,
    v_hbm,
    kt_hbm,
    vt_hbm,
    beta_hbm,
    decay_hbm,
    maps_hbm,
    answer_hbm,
    keys_hbm,
    rim_ref,
    k_ref,
    v_ref,
    kt_ref,
    vt_ref,
    beta_ref,
    decay_ref,
    maps_ref,
    answer_ref,
    keys_ref,
    sems,
    out_sems,
):
    copies = fetch(
        (
            (decay_hbm, decay_ref),
            (beta_hbm, beta_ref),
            (rim_hbm, rim_ref),
            (kt_hbm, kt_ref),
            (k_hbm, k_ref),
            (vt_hbm, vt_ref),
            (v_hbm, v_ref),
        ),
        sems,
    )
    sends = []

    def send(src, dst):
        copy = pltpu.make_async_copy(src, dst, out_sems.at[len(sends)])
        copy.start()
        sends.append(copy)

    rows = k_ref.shape[0]
    heads = beta_ref.shape[0]
    k_cols = k_ref.shape[1]
    key_heads = k_cols // DK
    ratio = heads // key_heads
    side = rows // 2

    row, col = triangle((side, side))
    strict = row > col
    eye = jnp.where(row == col, 1.0, 0.0)
    wide_row, wide_col = triangle((rows, rows))
    ones = jnp.where(wide_row >= wide_col, 1.0, 0.0).astype(BF16)
    eye_b = jnp.where(wide_row == wide_col, 1.0, 0.0).astype(BF16)

    copies[0].wait()
    copies[1].wait()
    both = jnp.concatenate([decay_ref[...], beta_ref[...]], axis=0)
    upto_col = exact_sums(ones, both, NT, False)
    upto_row = exact_sums(ones, both, NT, True)
    plain_col = exact_sums(eye_b, both, NT, False)

    keys = []
    inner = []
    for copy in copies[2:5]:
        copy.wait()
    for g in range(key_heads):
        cols = slice(g * DK, (g + 1) * DK)
        k = conv(rim_ref[:, k_cols + g * DK : k_cols + (g + 1) * DK], k_ref[:, cols], kt_ref[:, cols])
        k = k * lax.rsqrt(jnp.sum(k * k, axis=-1, keepdims=True) + 1e-06)
        keys.append(k)
        parts = split(k)
        keys_ref[:, cols] = parts[0]
        inner.append(dot3(parts, parts, NT))
    send(keys_ref, keys_hbm)

    spans = (slice(0, side), slice(side, rows))
    lowers = []
    solved = []
    for h in range(heads):
        g = h // ratio
        part = {}
        for i, j in ((0, 0), (1, 0), (1, 1)):
            spread = upto_col[spans[i], h : h + 1] - upto_row[h : h + 1, spans[j]]
            scaled = plain_col[spans[i], heads + h : heads + h + 1] * jnp.exp(jnp.minimum(spread, 0.0))
            value = scaled * inner[g][spans[i], spans[j]]
            part[i, j] = jnp.where(strict, value, 0.0) if i == j else value
        lowers.append({key: split(value) for key, value in part.items()})
        solved.append([eye - jnp.where(row // 2 == col // 2, part[d, d], 0.0) for d in range(2)])

    copies[5].wait()
    copies[6].wait()
    half = DV // 2
    lasts = [upto_col[rows - 1 : rows, h : h + 1] for h in range(heads)]
    rights = []
    tails = []

    def ready(h):
        g = h // ratio
        vcols = slice(h * DV, (h + 1) * DV)
        start = k_cols * 2 + h * DV
        v = conv(rim_ref[:, start : start + DV], v_ref[:, vcols], vt_ref[:, vcols])
        beta = plain_col[:, heads + h : heads + h + 1]
        reach = jnp.exp(upto_col[:, h : h + 1])
        rights.append(split(jnp.concatenate([(beta * reach) * keys[g], beta * v], axis=1)))
        tails.append(split(jnp.exp(lasts[h] - upto_col[:, h : h + 1]) * keys[g]))

    size = 2
    while size < side:
        pick = (row // (2 * size) == col // (2 * size)) & (row // size > col // size)
        middle = []
        for h in range(heads):
            for d in range(2):
                off = [jnp.where(pick, part, jnp.zeros_like(part)) for part in lowers[h][d, d]]
                x = split(solved[h][d])
                middle.append((x, packed(wide_left(off), wide_right(x))))
        if len(rights) < heads:
            ready(len(rights))
        for h in range(heads):
            for d in range(2):
                x, y = middle[2 * h + d]
                solved[h][d] = solved[h][d] - packed(wide_left(x), wide_right(split(y)))
        size *= 2
    while len(rights) < heads:
        ready(len(rights))

    done = [[split(x) for x in pair] for pair in solved]
    middle = [packed(wide_left(lowers[h][1, 0]), wide_right(done[h][0])) for h in range(heads)]
    firsts = []
    for h in range(heads):
        x0, right = done[h][0], rights[h]
        doubled = jnp.concatenate([right[0][:side]] * 2, axis=0)
        firsts.append(dot(wide_left(x0), doubled) + dot(x0[0], right[1][:side]))
    corners = [split(-packed(wide_left(done[h][1]), wide_right(split(middle[h])))) for h in range(heads)]
    answers = []
    for h in range(heads):
        bottom = [jnp.concatenate([corners[h][i], done[h][1][i]], axis=1) for i in range(2)]
        answers.append(split(jnp.concatenate([firsts[h], dot3(bottom, rights[h])], axis=0)))
        answer_ref[h] = answers[h][0]
        send(answer_ref.at[h], answer_hbm.at[h])
    folds = []
    for h in range(heads):
        folded = dot(answers[h][0], jnp.concatenate(tails[h], axis=1), TN)
        folds.append(folded[:, :DK] + (folded[:, DK:] + dot(answers[h][1], tails[h][0], TN)))
    for h in range(heads):
        square = jnp.where(row[:DK, :DK] == col[:DK, :DK], jnp.exp(lasts[h]), 0.0)
        step_map = (square - folds[h][:DK]).astype(BF16)
        added = folds[h][DK:].astype(BF16)
        maps_ref[2 * h, :DK] = step_map
        maps_ref[2 * h + 1, :DK] = step_map
        maps_ref[2 * h, DK:] = added[:half]
        maps_ref[2 * h + 1, DK:] = added[half:]
        send(maps_ref.at[pl.ds(2 * h, 2)], maps_hbm.at[pl.ds(2 * h, 2)])
    for copy in sends:
        copy.wait()


def reach_kernel(rim_ref, q_ref, qt_ref, decay_ref, answer_ref, keys_ref, base_ref, reach_ref):
    rows = q_ref.shape[0]
    heads = decay_ref.shape[0]
    key_heads = q_ref.shape[1] // DK
    ratio = heads // key_heads
    side = rows // 2
    row, col = triangle((side, side))
    lower = row >= col
    wide_row, wide_col = triangle((rows, rows))
    ones = jnp.where(wide_row >= wide_col, 1.0, 0.0).astype(BF16)
    both = jnp.concatenate([decay_ref[...], decay_ref[...]], axis=0)
    upto_col = exact_sums(ones, both, NT, False)
    upto_row = exact_sums(ones, both, NT, True)
    queries = []
    cross = []
    for g in range(key_heads):
        cols = slice(g * DK, (g + 1) * DK)
        q = conv(rim_ref[:, cols], q_ref[:, cols], qt_ref[:, cols])
        queries.append(q)
        cross.append(dot(q.astype(BF16), keys_ref[:, cols], NT))
    spans = (slice(0, side), slice(side, rows))
    for h in range(heads):
        g = h // ratio
        vcols = slice(h * DV, (h + 1) * DV)
        sims = {}
        for i, j in ((0, 0), (1, 0), (1, 1)):
            spread = upto_col[spans[i], h : h + 1] - upto_row[h : h + 1, spans[j]]
            value = jnp.exp(jnp.minimum(spread, 0.0)) * cross[g][spans[i], spans[j]]
            sims[i, j] = (jnp.where(lower, value, 0.0) if i == j else value).astype(BF16)
        for i in range(2):
            left = sims[0, 0] if i == 0 else jnp.concatenate([sims[1, 0], sims[1, 1]], axis=1)
            emitted = dot(left, answer_ref[h, : left.shape[1]])
            base_ref[spans[i], vcols] = emitted[:, DK:]
            gone = jnp.exp(upto_col[spans[i], h : h + 1])
            reach_ref[spans[i], vcols] = (gone * queries[g][spans[i]] - emitted[:, :DK]).astype(BF16)


def line_kernel(maps_ref, prefix_ref, total_ref):
    count = maps_ref.shape[0]
    rows = maps_ref.shape[1]
    row = lax.broadcasted_iota(jnp.int32, (rows, DK), 0)
    col = lax.broadcasted_iota(jnp.int32, (rows, DK), 1)
    prefix_ref[0] = jnp.where(row == col, 1.0, 0.0)
    running = maps_ref[0].astype(F32)
    for place in range(1, count):
        prefix_ref[place] = running
        added = jnp.where(row >= DK, maps_ref[place].astype(F32), 0.0)
        running = dot2(split(running), maps_ref[place, :DK]) + added
    total = running.astype(BF16)
    for place in range(total_ref.shape[0]):
        total_ref[place] = total


def start_kernel(totals_ref, prefix_ref, state_ref):
    count = totals_ref.shape[0]
    place = lax.axis_index("z")
    half = totals_ref.shape[1] - DK
    state = jnp.zeros((half, DK), F32)
    for earlier in range(count - 1):
        later = totals_ref[earlier, DK:].astype(F32)
        if earlier > 0:
            later = later + dot2(split(state), totals_ref[earlier, :DK])
        state = jnp.where(earlier < place, later, state)
    parts = split(state)
    for step in range(prefix_ref.shape[0]):
        moved = prefix_ref[step, DK:] + dot3(parts, split(prefix_ref[step, :DK]))
        state_ref[step] = moved.astype(BF16)


def finish_kernel(base_ref, reach_ref, state_ref, gate_ref, gain_ref, weight_ref, out_ref):
    heads = base_ref.shape[1] // DV
    gain = gain_ref[...]
    pieces = []
    for h in range(heads):
        cols = slice(h * DV, (h + 1) * DV)
        core = base_ref[:, cols] + dot(reach_ref[:, cols], state_ref[h], NT)
        scale = lax.rsqrt(jnp.mean(core * core, axis=-1, keepdims=True) + 1e-06)
        gate = silu(gate_ref[:, cols].astype(F32))
        pieces.append((core * scale * gain * gate).astype(BF16))
    gated = jnp.concatenate(pieces, axis=1)
    width = 512
    for start in range(0, out_ref.shape[1], width):
        cols = slice(start, start + width)
        out_ref[:, cols] = dot(gated, weight_ref[:, cols]).astype(BF16)


def call(kernel, outs, *args, hbm=(), hbm_outs=False, scratch=(), limit=24):
    vmem = pl.BlockSpec(memory_space=pltpu.VMEM)
    far = pl.BlockSpec(memory_space=pltpu.HBM)
    return pl.pallas_call(
        kernel,
        out_shape=outs,
        in_specs=[far if i in hbm else vmem for i in range(len(args))],
        out_specs=jax.tree.map(lambda _: far if hbm_outs else vmem, outs),
        scratch_shapes=list(scratch),
        compiler_params=pltpu.CompilerParams(vmem_limit_bytes=limit << 20),
        interpret=pltpu.InterpretParams() if INTERPRET else False,
    )(*args)


def local(
    nz,
    ny,
    ntp,
    query_in,
    key_in,
    value_in,
    gate_values,
    query_conv,
    key_conv,
    value_conv,
    beta_rate,
    log_decay,
    norm_gain,
    out_weight,
):
    shape = jax.ShapeDtypeStruct
    rows = query_in.shape[0]
    heads = beta_rate.shape[0]
    rim = 16
    raw = (query_in, key_in, value_in)
    tail_rows = call(
        tail_kernel,
        shape((rim, sum(a.shape[1] for a in raw)), BF16),
        *raw,
        hbm=range(3),
        scratch=(pltpu.SemaphoreType.DMA((3,)),),
        limit=60,
    )
    count = nz * ny
    rim_rows = lax.ppermute(tail_rows, ("z", "y"), [(i, i + 1) for i in range(count - 1)])

    half = DV // 2
    inputs = (rim_rows, key_in, value_in, key_conv, value_conv, beta_rate, log_decay)
    made = (
        shape((2 * heads, DK + half, DK), BF16),
        shape((heads, rows, DK + DV), BF16),
        shape(key_in.shape, BF16),
    )
    maps, answer, keys = call(
        prepare_kernel,
        made,
        *inputs,
        hbm=range(len(inputs)),
        hbm_outs=True,
        scratch=(
            *(pltpu.VMEM(a.shape, a.dtype) for a in (*inputs, *made)),
            pltpu.SemaphoreType.DMA((len(inputs),)),
            pltpu.SemaphoreType.DMA((2 * heads + 1,)),
        ),
        limit=60,
    )
    base, reach = call(
        reach_kernel,
        (shape((rows, heads * DV), F32), shape((rows, heads * DK), BF16)),
        rim_rows,
        query_in,
        query_conv,
        log_decay,
        answer,
        keys,
        limit=REACH_LIMIT,
    )
    maps = lax.all_to_all(maps, "y", 0, 0, tiled=True)
    maps, base, reach = lax.optimization_barrier((maps, base, reach))
    prefix, totals = call(
        line_kernel, (shape((ny, DK + half, DK), F32), shape((nz, DK + half, DK), BF16)), maps
    )
    totals = lax.all_to_all(totals, "z", 0, 0, tiled=True)
    states = call(start_kernel, shape((ny, half, DK), BF16), totals, prefix)
    states = lax.all_to_all(states, "y", 0, 0, tiled=True)
    partial = call(
        finish_kernel,
        shape((rows, out_weight.shape[1]), BF16),
        base,
        reach,
        states.reshape(heads, DV, DK),
        gate_values,
        norm_gain.reshape(1, DV),
        out_weight,
    )
    parts = lax.all_to_all(partial.reshape(ntp, rows // ntp, -1), "tp", 0, 0, tiled=True)
    return jnp.sum(parts.astype(F32), axis=0).astype(BF16)


def build(mesh):
    nz, ny, ntp = mesh.devices.shape
    ctx = ("z", "y")
    return jax.shard_map(
        functools.partial(local, nz, ny, ntp),
        mesh=mesh,
        in_specs=(
            P(ctx, "tp"),
            P(ctx, "tp"),
            P(ctx, "tp"),
            P(ctx, "tp"),
            P(None, "tp"),
            P(None, "tp"),
            P(None, "tp"),
            P("tp", ctx),
            P("tp", ctx),
            P(),
            P("tp", None),
        ),
        out_specs=P((*ctx, "tp"), None),
        check_vma=False,
    )


def solution(mesh):
    return build(Mesh(mesh.devices.reshape(8, 8, 8), ("z", "y", "tp")))
```

time: 109 us -> 95.8 us (0.88)
  local copies, waits for them, and re-layouts: 11.8 us -> 0.63 us
  starting transfers between devices: 14.2 us -> 12.5 us
  Pallas kernels: 12.8 us -> 13.9 us
    unnamed x32 -> x12, local copies, waits for them, and re-layouts: 9.71 us -> 0.63 us
    all_to_all x1, blocking collectives: 13.9 us -> 11.7 us  [local(): states = lax.all_to_all(states, 'y', 0, 0, tiled=True)]
    slice x3 -> x0, local copies, waits for them, and re-layouts: 2.13 us -> none  [local(): a[rows - rim:]]
    all_to_all x1, starting transfers between devices: 10 us -> 8.52 us  [local(): maps = lax.all_to_all(maps, 'y', 0, 0, tiled=True)]
    all_to_all x1, blocking collectives: 23.1 us -> 24.4 us  [local(): lax.all_to_all(partial.reshape(ntp, rows // ntp, -1), 'tp', 0, 0, tiled=T...]
    all_to_all x1, waiting for transfers between devices: 10.8 us -> 9.55 us  [local(): maps = lax.all_to_all(maps, 'y', 0, 0, tiled=True)]
    pallas_call x4 -> x6, Pallas kernels: 12.8 us -> 13.9 us  [call(): pl.pallas_call(kernel, out_shape=outs, in_specs=[far if i in hbm else vme...]
  transfers between devices with their start and end apart: 2 -> 2, of which waited for: 2 -> 2; matrix products, arithmetic and copies ran while one was open for 0% -> 0% of each run, Pallas kernels for 0% -> 3%
where the time goes in v2:
time: 95.8 us; the launch traced here: 95.4 us
  blocking collectives  56.5 us (59%)
  Pallas kernels  13.9 us (15%)
  starting transfers between devices  12.5 us (13%)
  waiting for transfers between devices  10.9 us (11%)
    all_to_all x1, blocking collectives, local(): lax.all_to_all(partial.reshape(ntp, rows // ntp, -1), 'tp', 0, 0, tiled=T...  24.4 us
    all_to_all x1, blocking collectives, local(): totals = lax.all_to_all(totals, 'z', 0, 0, tiled=True)  20.4 us
    pallas_call x6, Pallas kernels, call(): pl.pallas_call(kernel, out_shape=outs, in_specs=[far if i in hbm else vme...  13.9 us
    all_to_all x1, blocking collectives, local(): states = lax.all_to_all(states, 'y', 0, 0, tiled=True)  11.7 us
    all_to_all x1, waiting for transfers between devices, local(): maps = lax.all_to_all(maps, 'y', 0, 0, tiled=True)  9.55 us
    all_to_all x1, starting transfers between devices, local(): maps = lax.all_to_all(maps, 'y', 0, 0, tiled=True)  8.52 us
    ppermute x1, starting transfers between devices, local(): lax.ppermute(tail_rows, ('z', 'y'), [(i, i + 1) for i in range(count - 1)])  4.02 us
  transfers between devices with their start and end apart: 2, of which 2 were waited for; matrix products, arithmetic and copies ran while one was open for 0% of the time, Pallas kernels for 3%

profile of v2, /device:TPU:1, one launch (start us, length us, event | category | flops | bytes accessed | tf_op | source)
XLA Modules:
  0.0 95.4 jit_solution(7239646358306946990)
XLA Ops:
  0.0 1.4 %shard_map.109 = bf16[16,1024]{1,0:T(8,128)(2,1)} custom-call(bf16[256,256]{1,0:T(8,128)(2,1)} %q_ref.1, bf16[256,256]{1,0:T(8,128)(2,1)} %k_hbm.3, bf16[256,512]{1,0:T(8,128)(2,1)} %v_hbm.3), custom_call_target="tpu_custom_call" | custom-call | tf_op jit(solution)/shard_map/pallas_call | solution.py:355
  1.4 4.0 %collective-permute-start = (bf16[16,1024]{1,0:T(8,128)(2,1)}, bf16[16,1024]{1,0:T(8,128)(2,1)S(1)}, u32[]{:S(2)}, u32[]{:S(2)}) collective-permute-start(bf16[16,1024]{1,0:T(8,128)(2,1)} %shard_map.109), channel_id=1, source_target_pairs={{0,8},{8,16},{16,24},{24,32},{32,40},{40,48},{48,56},{56,64},{64,7... | collective-permute-start | bytes 98312 | tf_op jit(solution)/shard_map/ppermute | solution.py:396
  5.4 1.3 %collective-permute-done.rim_hbm.rim_ref = bf16[16,1024]{1,0:T(8,128)(2,1)S(1)} collective-permute-done((bf16[16,1024]{1,0:T(8,128)(2,1)}, bf16[16,1024]{1,0:T(8,128)(2,1)S(1)}, u32[]{:S(2)}, u32[]{:S(2)}) %collective-permute-start) | collective-permute-done | bytes 32800 | tf_op jit(solution)/shard_map/ppermute | solution.py:396
  6.7 0.0 copy-start.5
  6.7 0.6 copy-done.5
  7.3 6.5 %shard_map.110 = (bf16[8,192,128]{2,1,0:T(8,128)(2,1)}, bf16[4,256,256]{2,1,0:T(8,128)(2,1)}, bf16[256,256]{1,0:T(8,128)(2,1)}) custom-call(bf16[16,1024]{1,0:T(8,128)(2,1)} %copy-done.5, bf16[256,256]{1,0:T(8,128)(2,1)} %k_hbm.3, bf16[256,512]{1,0:T(8,128)(2,1)} %v_hbm.3, bf16[4,256]{1,0:T(4,128)(2,1)} %kt_hbm.1, bf16[4,512]{1,0:T(4,128)(2,1)} %vt_hbm.1, ...), custom_call_target="tpu_custom_call" | custom-call | tf_op jit(solution)/shard_map/pallas_call | solution.py:355
  13.8 0.0 copy-start
  13.8 0.0 copy-start.2
  13.9 0.0 copy-start.4
  13.9 8.5 %all-to-all-start = ((bf16[8,192,128]{2,1,0:T(8,128)(2,1)}), bf16[8,192,128]{2,1,0:T(8,128)(2,1)S(1)}, u32[]{:S(2)}, u32[]{:S(2)}) async-start(bf16[8,192,128]{2,1,0:T(8,128)(2,1)} %get-tuple-element.15), calls=%async_computation | async-start | bytes 786432 | tf_op jit(solution)/shard_map/all_to_all | solution.py:429
  22.4 2.8 %shard_map.111 = (f32[256,512]{1,0:T(8,128)}, bf16[256,512]{1,0:T(8,128)(2,1)}) custom-call(bf16[16,1024]{1,0:T(8,128)(2,1)} %copy-done.5, bf16[256,256]{1,0:T(8,128)(2,1)} %q_ref.1, bf16[4,256]{1,0:T(4,128)(2,1)} %qt_ref.1, f32[4,256]{1,0:T(4,128)} %decay_ref.1, bf16[4,256,256]{2,1,0:T(8,128)(2,1)} %get-tuple-element.16.answer_ref, ...), custom_call_target="tpu_custom_call" | custom-call | tf_op jit(solution)/shard_map/pallas_call | solution.py:355
  25.2 0.0 copy-start.1
  25.2 0.0 copy-start.3
  25.2 9.5 %all-to-all-done.maps_ref = bf16[8,192,128]{2,1,0:T(8,128)(2,1)S(1)} async-done(((bf16[8,192,128]{2,1,0:T(8,128)(2,1)}), bf16[8,192,128]{2,1,0:T(8,128)(2,1)S(1)}, u32[]{:S(2)}, u32[]{:S(2)}) %all-to-all-start) | async-done | bytes 393248 | tf_op jit(solution)/shard_map/all_to_all | solution.py:429
  34.7 1.1 %shard_map.112 = (f32[8,192,128]{2,1,0:T(8,128)S(1)}, bf16[8,192,128]{2,1,0:T(8,128)(2,1)S(1)}) custom-call(bf16[8,192,128]{2,1,0:T(8,128)(2,1)S(1)} %all-to-all-done.maps_ref), custom_call_target="tpu_custom_call" | custom-call | tf_op jit(solution)/shard_map/pallas_call | solution.py:355
  35.8 20.4 %all_to_all.20.totals_ref = bf16[8,192,128]{2,1,0:T(8,128)(2,1)S(1)} all-to-all(bf16[8,192,128]{2,1,0:T(8,128)(2,1)S(1)} %get-tuple-element.23), channel_id=1, replica_groups=mesh['z'=8,'y'=8,'tp'=8] {'z'}, dimensions={0} | all-to-all | bytes 786432 | tf_op jit(solution)/shard_map/all_to_all | solution.py:434
  56.2 1.2 %shard_map.113 = bf16[8,64,128]{2,1,0:T(8,128)(2,1)S(1)} custom-call(bf16[8,192,128]{2,1,0:T(8,128)(2,1)S(1)} %all_to_all.20.totals_ref, f32[8,192,128]{2,1,0:T(8,128)S(1)} %get-tuple-element.24.prefix_ref), custom_call_target="tpu_custom_call" | custom-call | tf_op jit(solution)/shard_map/pallas_call | solution.py:355
  57.4 11.7 %all_to_all.21 = bf16[8,64,128]{2,1,0:T(8,128)(2,1)S(1)} all-to-all(bf16[8,64,128]{2,1,0:T(8,128)(2,1)S(1)} %shard_map.113), channel_id=1, replica_groups=mesh['z'=8,'y'=8,'tp'=8] {'y'}, dimensions={0} | all-to-all | bytes 262144 | tf_op jit(solution)/shard_map/all_to_all | solution.py:436
  69.1 0.0 copy-done
  69.1 0.0 copy-done.2
  69.1 0.0 copy-done.4
  69.1 0.0 copy-done.1
  69.1 0.0 copy-done.3
  69.1 1.0 %shard_map.114 = bf16[256,2048]{1,0:T(8,128)(2,1)S(1)} custom-call(f32[256,512]{1,0:T(8,128)S(1)} %copy-done.1, bf16[256,512]{1,0:T(8,128)(2,1)S(1)} %copy-done.3, bf16[4,128,128]{2,1,0:T(8,128)(2,1)S(1)} %bitcast.4, bf16[256,512]{1,0:T(8,128)(2,1)S(1)} %copy-done.2, f32[1,128]{1,0:T(1,128)S(1)} %bitcast.5, bf16[512,2048]{1,0:T(8,128)(2,1)S(1)} %copy-done), custom_call_target="tpu_custom_call" | custom-call | tf_op jit(solution)/shard_map/pallas_call | solution.py:355
  70.2 24.4 %all_to_all.22 = bf16[8,32,2048]{2,1,0:T(8,128)(2,1)S(1)} all-to-all(bf16[8,32,2048]{2,1,0:T(8,128)(2,1)S(1)} %bitcast.3), channel_id=1, replica_groups=mesh['z'=8,'y'=8,'tp'=8] {'tp'}, dimensions={0} | all-to-all | bytes 2097152 | tf_op jit(solution)/shard_map/all_to_all | solution.py:447
  94.6 0.8 reduce_sum.12
Async XLA Ops:
  1.4 5.3 %collective-permute-start = (bf16[16,1024]{1,0:T(8,128)(2,1)}, bf16[16,1024]{1,0:T(8,128)(2,1)S(1)}, u32[]{:S(2)}, u32[]{:S(2)}) collective-permute-start(bf16[16,1024]{1,0:T(8,128)(2,1)} %shard_map.109), channel_id=1, source_target_pairs={{0,8},{8,16},{16,24},{24,32},{32,40},{40,48},{48,56},{56,64},{64,7... | collective-permute-start | bytes 98312 | tf_op jit(solution)/shard_map/ppermute | solution.py:396
  6.7 0.6 copy-start.5
  13.8 55.3 %copy-start = (bf16[512,2048]{1,0:T(8,128)(2,1)S(1)}, bf16[512,2048]{1,0:T(8,128)(2,1)}, u32[]{:S(2)}) copy-start(bf16[512,2048]{1,0:T(8,128)(2,1)} %weight_ref.1) | copy-start | bytes 6291460
  13.8 55.3 %copy-start.2 = (bf16[256,512]{1,0:T(8,128)(2,1)S(1)}, bf16[256,512]{1,0:T(8,128)(2,1)}, u32[]{:S(2)}) copy-start(bf16[256,512]{1,0:T(8,128)(2,1)} %gate_ref.1) | copy-start | bytes 786436
  13.9 55.3 %copy-start.4 = (f32[128]{0:T(128)S(1)}, f32[128]{0:T(128)}, u32[]{:S(2)}) copy-start(f32[128]{0:T(128)} %param.20) | copy-start | bytes 1540
  13.9 20.8 %all-to-all-start = ((bf16[8,192,128]{2,1,0:T(8,128)(2,1)}), bf16[8,192,128]{2,1,0:T(8,128)(2,1)S(1)}, u32[]{:S(2)}, u32[]{:S(2)}) async-start(bf16[8,192,128]{2,1,0:T(8,128)(2,1)} %get-tuple-element.15), calls=%async_computation | async-start | bytes 786432 | tf_op jit(solution)/shard_map/all_to_all | solution.py:429
  25.2 44.0 %copy-start.1 = (f32[256,512]{1,0:T(8,128)S(1)}, f32[256,512]{1,0:T(8,128)}, u32[]{:S(2)}) copy-start(f32[256,512]{1,0:T(8,128)} %get-tuple-element.20.base_ref) | copy-start | bytes 1572868
  25.2 44.0 %copy-start.3 = (bf16[256,512]{1,0:T(8,128)(2,1)S(1)}, bf16[256,512]{1,0:T(8,128)(2,1)}, u32[]{:S(2)}) copy-start(bf16[256,512]{1,0:T(8,128)(2,1)} %get-tuple-element.21.reach_ref) | copy-start | bytes 786436

commit v3 on v2

--- a/solution.py
+++ b/solution.py
@@ -95,48 +95,138 @@
     return row, col
 
 
-def exact_sums(left, value, dims, swap):
-    high = value.astype(BF16)
-    rest = value - high.astype(F32)
-    mid = rest.astype(BF16)
-    low = (rest - mid.astype(F32)).astype(BF16)
-    parts = [dot(p, left, dims) if swap else dot(left, p, dims) for p in (high, mid, low)]
-    return parts[0] + (parts[1] + parts[2])
-
-
-def prepare_kernel(
-    rim_hbm,
+def pieces(value):
+    high = value.astype(BF16).astype(F32)
+    rest = value - high
+    mid = rest.astype(BF16).astype(F32)
+    return jnp.concatenate([high, mid, rest - mid], axis=0).astype(BF16)
+
+
+def column_sums(left, parts):
+    wide = dot(left, parts, NT)
+    count = wide.shape[1] // 3
+    return wide[:, :count] + (wide[:, count : 2 * count] + wide[:, 2 * count :])
+
+
+def row_sums(left, parts):
+    tall = dot(parts, left, NT)
+    count = tall.shape[0] // 3
+    return tall[:count] + (tall[count : 2 * count] + tall[2 * count :])
+
+
+def clock(decay_ref, beta_ref, rows):
+    row, col = triangle((rows, rows))
+    ones = jnp.where(row >= col, 1.0, 0.0).astype(BF16)
+    eye = jnp.where(row == col, 1.0, 0.0).astype(BF16)
+    parts = pieces(jnp.concatenate([decay_ref[...], beta_ref[...]], axis=0))
+    return column_sums(ones, parts), row_sums(ones, parts), column_sums(eye, parts)
+
+
+def lower_block(upto_col, upto_row, plain_col, inner, h, heads, rows, cols):
+    spread = upto_col[rows, h : h + 1] - upto_row[h : h + 1, cols]
+    scaled = plain_col[rows, heads + h : heads + h + 1] * jnp.exp(jnp.minimum(spread, 0.0))
+    return scaled * inner
+
+
+def unit(rows_of_keys):
+    return rows_of_keys * lax.rsqrt(jnp.sum(rows_of_keys * rows_of_keys, axis=-1, keepdims=True) + 1e-06)
+
+
+def level_masks(side):
+    row, col = triangle((side, side))
+    size = 2
+    while size < side:
+        yield (row // (2 * size) == col // (2 * size)) & (row // size > col // size)
+        size *= 2
+
+
+def start_inverse(lower):
+    row, col = triangle(lower.shape)
+    return jnp.where(row == col, 1.0, 0.0) - jnp.where(row // 2 == col // 2, lower, 0.0)
+
+
+def half_level(pick, lower, solved):
+    off = [jnp.where(pick, part, jnp.zeros_like(part)) for part in lower]
+    x = split(solved)
+    return x, packed(wide_left(off), wide_right(x))
+
+
+def first_kernel(
     k_hbm,
     v_hbm,
     kt_hbm,
     vt_hbm,
-    beta_hbm,
-    decay_hbm,
-    maps_hbm,
-    answer_hbm,
     keys_hbm,
-    rim_ref,
+    values_hbm,
     k_ref,
     v_ref,
     kt_ref,
     vt_ref,
+    keys_ref,
+    values_ref,
+    sems,
+    out_sems,
+):
+    copies = fetch(((kt_hbm, kt_ref), (k_hbm, k_ref), (vt_hbm, vt_ref), (v_hbm, v_ref)), sems)
+    empty = jnp.zeros((16, DK), BF16)
+    copies[0].wait()
+    copies[1].wait()
+    for start in range(0, k_ref.shape[1], DK):
+        cols = slice(start, start + DK)
+        keys_ref[:, cols] = unit(conv(empty, k_ref[:, cols], kt_ref[:, cols]))
+    sends = [pltpu.make_async_copy(keys_ref, keys_hbm, out_sems.at[0])]
+    sends[0].start()
+    copies[2].wait()
+    copies[3].wait()
+    for start in range(0, v_ref.shape[1], DV):
+        cols = slice(start, start + DV)
+        values_ref[:, cols] = conv(empty, v_ref[:, cols], vt_ref[:, cols])
+    sends.append(pltpu.make_async_copy(values_ref, values_hbm, out_sems.at[1]))
+    sends[1].start()
+    for copy in sends:
+        copy.wait()
+
+
+def prepare_kernel(
+    rim_hbm,
+    kt_hbm,
+    vt_hbm,
+    beta_hbm,
+    decay_hbm,
+    keys_hbm,
+    values_hbm,
+    k_hbm,
+    v_hbm,
+    maps_hbm,
+    answer_hbm,
+    keys_out_hbm,
+    rim_ref,
+    kt_ref,
+    vt_ref,
     beta_ref,
     decay_ref,
+    made_keys_ref,
+    made_values_ref,
+    k_ref,
+    v_ref,
     maps_ref,
     answer_ref,
     keys_ref,
     sems,
     out_sems,
 ):
+    rim = rim_ref.shape[0]
     copies = fetch(
         (
             (decay_hbm, decay_ref),
             (beta_hbm, beta_ref),
             (rim_hbm, rim_ref),
             (kt_hbm, kt_ref),
-            (k_hbm, k_ref),
+            (k_hbm.at[pl.ds(0, rim)], k_ref),
+            (keys_hbm, made_keys_ref),
             (vt_hbm, vt_ref),
-            (v_hbm, v_ref),
+            (v_hbm.at[pl.ds(0, rim)], v_ref),
+            (values_hbm, made_values_ref),
         ),
         sems,
     )
@@ -147,57 +237,46 @@
         copy.start()
         sends.append(copy)
 
-    rows = k_ref.shape[0]
+    rows = made_keys_ref.shape[0]
     heads = beta_ref.shape[0]
-    k_cols = k_ref.shape[1]
+    k_cols = made_keys_ref.shape[1]
     key_heads = k_cols // DK
     ratio = heads // key_heads
     side = rows // 2
-
     row, col = triangle((side, side))
-    strict = row > col
-    eye = jnp.where(row == col, 1.0, 0.0)
-    wide_row, wide_col = triangle((rows, rows))
-    ones = jnp.where(wide_row >= wide_col, 1.0, 0.0).astype(BF16)
-    eye_b = jnp.where(wide_row == wide_col, 1.0, 0.0).astype(BF16)
 
     copies[0].wait()
     copies[1].wait()
-    both = jnp.concatenate([decay_ref[...], beta_ref[...]], axis=0)
-    upto_col = exact_sums(ones, both, NT, False)
-    upto_row = exact_sums(ones, both, NT, True)
-    plain_col = exact_sums(eye_b, both, NT, False)
+    upto_col, upto_row, plain_col = clock(decay_ref, beta_ref, rows)
 
     keys = []
     inner = []
-    for copy in copies[2:5]:
+    for copy in copies[2:6]:
         copy.wait()
     for g in range(key_heads):
         cols = slice(g * DK, (g + 1) * DK)
-        k = conv(rim_ref[:, k_cols + g * DK : k_cols + (g + 1) * DK], k_ref[:, cols], kt_ref[:, cols])
-        k = k * lax.rsqrt(jnp.sum(k * k, axis=-1, keepdims=True) + 1e-06)
+        top = unit(conv(rim_ref[:, k_cols + g * DK : k_cols + (g + 1) * DK], k_ref[:, cols], kt_ref[:, cols]))
+        k = jnp.concatenate([top, made_keys_ref[rim:, cols]], axis=0)
         keys.append(k)
         parts = split(k)
         keys_ref[:, cols] = parts[0]
         inner.append(dot3(parts, parts, NT))
-    send(keys_ref, keys_hbm)
+    send(keys_ref, keys_out_hbm)
 
     spans = (slice(0, side), slice(side, rows))
     lowers = []
     solved = []
     for h in range(heads):
-        g = h // ratio
         part = {}
         for i, j in ((0, 0), (1, 0), (1, 1)):
-            spread = upto_col[spans[i], h : h + 1] - upto_row[h : h + 1, spans[j]]
-            scaled = plain_col[spans[i], heads + h : heads + h + 1] * jnp.exp(jnp.minimum(spread, 0.0))
-            value = scaled * inner[g][spans[i], spans[j]]
-            part[i, j] = jnp.where(strict, value, 0.0) if i == j else value
+            block = inner[h // ratio][spans[i], spans[j]]
+            value = lower_block(upto_col, upto_row, plain_col, block, h, heads, spans[i], spans[j])
+            part[i, j] = jnp.where(row > col, value, 0.0) if i == j else value
         lowers.append({key: split(value) for key, value in part.items()})
-        solved.append([eye - jnp.where(row // 2 == col // 2, part[d, d], 0.0) for d in range(2)])
-
-    copies[5].wait()
-    copies[6].wait()
+        solved.append([start_inverse(part[d, d]) for d in range(2)])
+
+    for copy in copies[6:]:
+        copy.wait()
     half = DV // 2
     lasts = [upto_col[rows - 1 : rows, h : h + 1] for h in range(heads)]
     rights = []
@@ -207,28 +286,20 @@
         g = h // ratio
         vcols = slice(h * DV, (h + 1) * DV)
         start = k_cols * 2 + h * DV
-        v = conv(rim_ref[:, start : start + DV], v_ref[:, vcols], vt_ref[:, vcols])
+        top = conv(rim_ref[:, start : start + DV], v_ref[:, vcols], vt_ref[:, vcols])
+        v = jnp.concatenate([top, made_values_ref[rim:, vcols]], axis=0)
         beta = plain_col[:, heads + h : heads + h + 1]
         reach = jnp.exp(upto_col[:, h : h + 1])
         rights.append(split(jnp.concatenate([(beta * reach) * keys[g], beta * v], axis=1)))
         tails.append(split(jnp.exp(lasts[h] - upto_col[:, h : h + 1]) * keys[g]))
 
-    size = 2
-    while size < side:
-        pick = (row // (2 * size) == col // (2 * size)) & (row // size > col // size)
-        middle = []
-        for h in range(heads):
-            for d in range(2):
-                off = [jnp.where(pick, part, jnp.zeros_like(part)) for part in lowers[h][d, d]]
-                x = split(solved[h][d])
-                middle.append((x, packed(wide_left(off), wide_right(x))))
+    units = [(h, d) for h in range(heads) for d in range(2)]
+    for pick in level_masks(side):
+        middle = [half_level(pick, lowers[h][d, d], solved[h][d]) for h, d in units]
         if len(rights) < heads:
             ready(len(rights))
-        for h in range(heads):
-            for d in range(2):
-                x, y = middle[2 * h + d]
-                solved[h][d] = solved[h][d] - packed(wide_left(x), wide_right(split(y)))
-        size *= 2
+        for (h, d), (x, y) in zip(units, middle):
+            solved[h][d] = solved[h][d] - packed(wide_left(x), wide_right(split(y)))
     while len(rights) < heads:
         ready(len(rights))
 
@@ -273,9 +344,9 @@
     lower = row >= col
     wide_row, wide_col = triangle((rows, rows))
     ones = jnp.where(wide_row >= wide_col, 1.0, 0.0).astype(BF16)
-    both = jnp.concatenate([decay_ref[...], decay_ref[...]], axis=0)
-    upto_col = exact_sums(ones, both, NT, False)
-    upto_row = exact_sums(ones, both, NT, True)
+    parts = pieces(jnp.concatenate([decay_ref[...], decay_ref[...]], axis=0))
+    upto_col = column_sums(ones, parts)
+    upto_row = row_sums(ones, parts)
     queries = []
     cross = []
     for g in range(key_heads):
@@ -349,7 +420,7 @@
         out_ref[:, cols] = dot(gated, weight_ref[:, cols]).astype(BF16)
 
 
-def call(kernel, outs, *args, hbm=(), hbm_outs=False, scratch=(), limit=24):
+def call(kernel, outs, *args, hbm=(), hbm_outs=False, scratch=(), limit=24, cost=None):
     vmem = pl.BlockSpec(memory_space=pltpu.VMEM)
     far = pl.BlockSpec(memory_space=pltpu.HBM)
     return pl.pallas_call(
@@ -358,6 +429,7 @@
         in_specs=[far if i in hbm else vmem for i in range(len(args))],
         out_specs=jax.tree.map(lambda _: far if hbm_outs else vmem, outs),
         scratch_shapes=list(scratch),
+        cost_estimate=cost,
         compiler_params=pltpu.CompilerParams(vmem_limit_bytes=limit << 20),
         interpret=pltpu.InterpretParams() if INTERPRET else False,
     )(*args)
@@ -396,12 +468,30 @@
     rim_rows = lax.ppermute(tail_rows, ("z", "y"), [(i, i + 1) for i in range(count - 1)])
 
     half = DV // 2
-    inputs = (rim_rows, key_in, value_in, key_conv, value_conv, beta_rate, log_decay)
+    small = (key_conv, value_conv, beta_rate, log_decay)
+    inputs = (key_in, value_in, key_conv, value_conv)
+    made = (shape(key_in.shape, F32), shape(value_in.shape, F32))
+    early = call(
+        first_kernel,
+        made,
+        *inputs,
+        hbm=range(len(inputs)),
+        hbm_outs=True,
+        scratch=(
+            *(pltpu.VMEM(a.shape, a.dtype) for a in (*inputs, *made)),
+            pltpu.SemaphoreType.DMA((len(inputs),)),
+            pltpu.SemaphoreType.DMA((len(made),)),
+        ),
+        limit=60,
+        cost=pl.CostEstimate(flops=10**8, bytes_accessed=3 << 20, transcendentals=1 << 20),
+    )
+    inputs = (rim_rows, *small, *early, key_in, value_in)
     made = (
         shape((2 * heads, DK + half, DK), BF16),
         shape((heads, rows, DK + DV), BF16),
         shape(key_in.shape, BF16),
     )
+    tops = (shape((rim, key_in.shape[1]), BF16), shape((rim, value_in.shape[1]), BF16))
     maps, answer, keys = call(
         prepare_kernel,
         made,
@@ -409,7 +499,7 @@
         hbm=range(len(inputs)),
         hbm_outs=True,
         scratch=(
-            *(pltpu.VMEM(a.shape, a.dtype) for a in (*inputs, *made)),
+            *(pltpu.VMEM(a.shape, a.dtype) for a in (*inputs[:-2], *tops, *made)),
             pltpu.SemaphoreType.DMA((len(inputs),)),
             pltpu.SemaphoreType.DMA((2 * heads + 1,)),
         ),

time: 95.8 us -> 95.2 us (level)
  Pallas kernels: 13.9 us -> 15.7 us
  waiting for transfers between devices: 10.9 us -> 9.54 us
  starting transfers between devices: 12.5 us -> 11.3 us
    pallas_call x6 -> x7, Pallas kernels: 13.9 us -> 15.7 us  [call(): pl.pallas_call(kernel, out_shape=outs, in_specs=[far if i in hbm else vme...]
    ppermute x1, waiting for transfers between devices: 1.32 us -> 0.01 us  [local(): lax.ppermute(tail_rows, ('z', 'y'), [(i, i + 1) for i in range(count - 1)])]
    all_to_all x1, starting transfers between devices: 8.52 us -> 7.32 us  [local(): maps = lax.all_to_all(maps, 'y', 0, 0, tiled=True)]
  transfers between devices with their start and end apart: 2 -> 2, of which waited for: 2 -> 1; matrix products, arithmetic and copies ran while one was open for 0% -> 0% of each run, Pallas kernels for 3% -> 6%
where the time goes in v3:
time: 95.2 us; the launch traced here: 94.7 us
  blocking collectives  56.6 us (59%)
  Pallas kernels  15.7 us (16%)
  starting transfers between devices  11.3 us (12%)
  waiting for transfers between devices  9.54 us (10%)
    all_to_all x1, blocking collectives, local(): lax.all_to_all(partial.reshape(ntp, rows // ntp, -1), 'tp', 0, 0, tiled=T...  24.4 us
    all_to_all x1, blocking collectives, local(): totals = lax.all_to_all(totals, 'z', 0, 0, tiled=True)  20.4 us
    pallas_call x7, Pallas kernels, call(): pl.pallas_call(kernel, out_shape=outs, in_specs=[far if i in hbm else vme...  15.7 us
    all_to_all x1, blocking collectives, local(): states = lax.all_to_all(states, 'y', 0, 0, tiled=True)  11.7 us
    all_to_all x1, waiting for transfers between devices, local(): maps = lax.all_to_all(maps, 'y', 0, 0, tiled=True)  9.54 us
    all_to_all x1, starting transfers between devices, local(): maps = lax.all_to_all(maps, 'y', 0, 0, tiled=True)  7.32 us
    ppermute x1, starting transfers between devices, local(): lax.ppermute(tail_rows, ('z', 'y'), [(i, i + 1) for i in range(count - 1)])  4.02 us
  transfers between devices with their start and end apart: 2, of which 1 were waited for; matrix products, arithmetic and copies ran while one was open for 0% of the time, Pallas kernels for 6%

profile of v3, /device:TPU:1, one launch (start us, length us, event | category | flops | bytes accessed | tf_op | source)
XLA Modules:
  0.0 94.7 jit_solution(8992439601118837793)
XLA Ops:
  0.0 1.4 %shard_map.109 = bf16[16,1024]{1,0:T(8,128)(2,1)} custom-call(bf16[256,256]{1,0:T(8,128)(2,1)} %q_ref.1, bf16[256,256]{1,0:T(8,128)(2,1)} %k_hbm.5, bf16[256,512]{1,0:T(8,128)(2,1)} %v_hbm.5), custom_call_target="tpu_custom_call" | custom-call | tf_op jit(solution)/shard_map/pallas_call | solution.py:426
  1.4 4.0 %collective-permute-start = (bf16[16,1024]{1,0:T(8,128)(2,1)}, bf16[16,1024]{1,0:T(8,128)(2,1)S(1)}, u32[]{:S(2)}, u32[]{:S(2)}) collective-permute-start(bf16[16,1024]{1,0:T(8,128)(2,1)} %shard_map.109), channel_id=1, source_target_pairs={{0,8},{8,16},{16,24},{24,32},{32,40},{40,48},{48,56},{56,64},{64,7... | collective-permute-start | bytes 98312 | tf_op jit(solution)/shard_map/ppermute | solution.py:468
  5.4 2.4 %shard_map.110 = (f32[256,256]{1,0:T(8,128)}, f32[256,512]{1,0:T(8,128)}) custom-call(bf16[256,256]{1,0:T(8,128)(2,1)} %k_hbm.5, bf16[256,512]{1,0:T(8,128)(2,1)} %v_hbm.5, bf16[4,256]{1,0:T(4,128)(2,1)} %kt_hbm.3, bf16[4,512]{1,0:T(4,128)(2,1)} %vt_hbm.3), custom_call_target="tpu_custom_call" | custom-call | flops 100000000 | bytes 3145728 | tf_op jit(solution)/shard_map/pallas_call | solution.py:426
  7.9 0.0 collective-permute-done.rim_hbm.rim_ref
  7.9 0.0 copy-start.5
  7.9 0.6 copy-done.5
  8.5 5.8 %shard_map.111 = (bf16[8,192,128]{2,1,0:T(8,128)(2,1)}, bf16[4,256,256]{2,1,0:T(8,128)(2,1)}, bf16[256,256]{1,0:T(8,128)(2,1)}) custom-call(bf16[16,1024]{1,0:T(8,128)(2,1)} %copy-done.5, bf16[4,256]{1,0:T(4,128)(2,1)} %kt_hbm.3, bf16[4,512]{1,0:T(4,128)(2,1)} %vt_hbm.3, f32[4,256]{1,0:T(4,128)} %beta_hbm.1, f32[4,256]{1,0:T(4,128)} %decay_ref.1, ...), custom_call_target="tpu_custom_call" | custom-call | tf_op jit(solution)/shard_map/pallas_call | solution.py:426
  14.3 0.0 copy-start
  14.3 0.0 copy-start.2
  14.3 0.0 copy-start.4
  14.4 7.3 %all-to-all-start = ((bf16[8,192,128]{2,1,0:T(8,128)(2,1)}), bf16[8,192,128]{2,1,0:T(8,128)(2,1)S(1)}, u32[]{:S(2)}, u32[]{:S(2)}) async-start(bf16[8,192,128]{2,1,0:T(8,128)(2,1)} %get-tuple-element.19), calls=%async_computation | async-start | bytes 786432 | tf_op jit(solution)/shard_map/all_to_all | solution.py:519
  21.7 2.8 %shard_map.112 = (f32[256,512]{1,0:T(8,128)}, bf16[256,512]{1,0:T(8,128)(2,1)}) custom-call(bf16[16,1024]{1,0:T(8,128)(2,1)} %copy-done.5, bf16[256,256]{1,0:T(8,128)(2,1)} %q_ref.1, bf16[4,256]{1,0:T(4,128)(2,1)} %qt_ref.1, f32[4,256]{1,0:T(4,128)} %decay_ref.1, bf16[4,256,256]{2,1,0:T(8,128)(2,1)} %get-tuple-element.20.answer_ref, ...), custom_call_target="tpu_custom_call" | custom-call | tf_op jit(solution)/shard_map/pallas_call | solution.py:426
  24.5 0.0 copy-start.1
  24.5 0.0 copy-start.3
  24.5 9.5 %all-to-all-done.maps_ref = bf16[8,192,128]{2,1,0:T(8,128)(2,1)S(1)} async-done(((bf16[8,192,128]{2,1,0:T(8,128)(2,1)}), bf16[8,192,128]{2,1,0:T(8,128)(2,1)S(1)}, u32[]{:S(2)}, u32[]{:S(2)}) %all-to-all-start) | async-done | bytes 393248 | tf_op jit(solution)/shard_map/all_to_all | solution.py:519
  34.0 1.1 %shard_map.113 = (f32[8,192,128]{2,1,0:T(8,128)S(1)}, bf16[8,192,128]{2,1,0:T(8,128)(2,1)S(1)}) custom-call(bf16[8,192,128]{2,1,0:T(8,128)(2,1)S(1)} %all-to-all-done.maps_ref), custom_call_target="tpu_custom_call" | custom-call | tf_op jit(solution)/shard_map/pallas_call | solution.py:426
  35.1 20.4 %all_to_all.20.totals_ref = bf16[8,192,128]{2,1,0:T(8,128)(2,1)S(1)} all-to-all(bf16[8,192,128]{2,1,0:T(8,128)(2,1)S(1)} %get-tuple-element.27), channel_id=1, replica_groups=mesh['z'=8,'y'=8,'tp'=8] {'z'}, dimensions={0} | all-to-all | bytes 786432 | tf_op jit(solution)/shard_map/all_to_all | solution.py:524
  55.5 1.2 %shard_map.114 = bf16[8,64,128]{2,1,0:T(8,128)(2,1)S(1)} custom-call(bf16[8,192,128]{2,1,0:T(8,128)(2,1)S(1)} %all_to_all.20.totals_ref, f32[8,192,128]{2,1,0:T(8,128)S(1)} %get-tuple-element.28.prefix_ref), custom_call_target="tpu_custom_call" | custom-call | tf_op jit(solution)/shard_map/pallas_call | solution.py:426
  56.7 11.7 %all_to_all.21 = bf16[8,64,128]{2,1,0:T(8,128)(2,1)S(1)} all-to-all(bf16[8,64,128]{2,1,0:T(8,128)(2,1)S(1)} %shard_map.114), channel_id=1, replica_groups=mesh['z'=8,'y'=8,'tp'=8] {'y'}, dimensions={0} | all-to-all | bytes 262144 | tf_op jit(solution)/shard_map/all_to_all | solution.py:526
  68.4 0.0 copy-done
  68.4 0.0 copy-done.2
  68.4 0.0 copy-done.4
  68.4 0.0 copy-done.1
  68.4 0.0 copy-done.3
  68.4 1.1 %shard_map.115 = bf16[256,2048]{1,0:T(8,128)(2,1)S(1)} custom-call(f32[256,512]{1,0:T(8,128)S(1)} %copy-done.1, bf16[256,512]{1,0:T(8,128)(2,1)S(1)} %copy-done.3, bf16[4,128,128]{2,1,0:T(8,128)(2,1)S(1)} %bitcast.4, bf16[256,512]{1,0:T(8,128)(2,1)S(1)} %copy-done.2, f32[1,128]{1,0:T(1,128)S(1)} %bitcast.5, bf16[512,2048]{1,0:T(8,128)(2,1)S(1)} %copy-done), custom_call_target="tpu_custom_call" | custom-call | tf_op jit(solution)/shard_map/pallas_call | solution.py:426
  69.5 24.4 %all_to_all.22 = bf16[8,32,2048]{2,1,0:T(8,128)(2,1)S(1)} all-to-all(bf16[8,32,2048]{2,1,0:T(8,128)(2,1)S(1)} %bitcast.3), channel_id=1, replica_groups=mesh['z'=8,'y'=8,'tp'=8] {'tp'}, dimensions={0} | all-to-all | bytes 2097152 | tf_op jit(solution)/shard_map/all_to_all | solution.py:537
  93.9 0.8 reduce_sum.12
Async XLA Ops:
  1.4 6.5 %collective-permute-start = (bf16[16,1024]{1,0:T(8,128)(2,1)}, bf16[16,1024]{1,0:T(8,128)(2,1)S(1)}, u32[]{:S(2)}, u32[]{:S(2)}) collective-permute-start(bf16[16,1024]{1,0:T(8,128)(2,1)} %shard_map.109), channel_id=1, source_target_pairs={{0,8},{8,16},{16,24},{24,32},{32,40},{40,48},{48,56},{56,64},{64,7... | collective-permute-start | bytes 98312 | tf_op jit(solution)/shard_map/ppermute | solution.py:468
  7.9 0.6 copy-start.5
  14.3 54.1 %copy-start = (bf16[512,2048]{1,0:T(8,128)(2,1)S(1)}, bf16[512,2048]{1,0:T(8,128)(2,1)}, u32[]{:S(2)}) copy-start(bf16[512,2048]{1,0:T(8,128)(2,1)} %weight_ref.1) | copy-start | bytes 6291460
  14.3 54.1 %copy-start.2 = (bf16[256,512]{1,0:T(8,128)(2,1)S(1)}, bf16[256,512]{1,0:T(8,128)(2,1)}, u32[]{:S(2)}) copy-start(bf16[256,512]{1,0:T(8,128)(2,1)} %gate_ref.1) | copy-start | bytes 786436
  14.3 54.1 %copy-start.4 = (f32[128]{0:T(128)S(1)}, f32[128]{0:T(128)}, u32[]{:S(2)}) copy-start(f32[128]{0:T(128)} %param.20) | copy-start | bytes 1540
  14.4 19.7 %all-to-all-start = ((bf16[8,192,128]{2,1,0:T(8,128)(2,1)}), bf16[8,192,128]{2,1,0:T(8,128)(2,1)S(1)}, u32[]{:S(2)}, u32[]{:S(2)}) async-start(bf16[8,192,128]{2,1,0:T(8,128)(2,1)} %get-tuple-element.19), calls=%async_computation | async-start | bytes 786432 | tf_op jit(solution)/shard_map/all_to_all | solution.py:519
  24.5 44.0 %copy-start.1 = (f32[256,512]{1,0:T(8,128)S(1)}, f32[256,512]{1,0:T(8,128)}, u32[]{:S(2)}) copy-start(f32[256,512]{1,0:T(8,128)} %get-tuple-element.24.base_ref) | copy-start | bytes 1572868
  24.5 44.0 %copy-start.3 = (bf16[256,512]{1,0:T(8,128)(2,1)S(1)}, bf16[256,512]{1,0:T(8,128)(2,1)}, u32[]{:S(2)}) copy-start(bf16[256,512]{1,0:T(8,128)(2,1)} %get-tuple-element.25.reach_ref) | copy-start | bytes 786436

commit v4 on v3

--- a/solution.py
+++ b/solution.py
@@ -259,7 +259,8 @@
         k = jnp.concatenate([top, made_keys_ref[rim:, cols]], axis=0)
         keys.append(k)
         parts = split(k)
-        keys_ref[:, cols] = parts[0]
+        for i in range(2):
+            keys_ref[i, :, cols] = parts[i]
         inner.append(dot3(parts, parts, NT))
     send(keys_ref, keys_out_hbm)
 
@@ -315,7 +316,8 @@
     for h in range(heads):
         bottom = [jnp.concatenate([corners[h][i], done[h][1][i]], axis=1) for i in range(2)]
         answers.append(split(jnp.concatenate([firsts[h], dot3(bottom, rights[h])], axis=0)))
-        answer_ref[h] = answers[h][0]
+        for i in range(2):
+            answer_ref[h, i] = answers[h][i]
         send(answer_ref.at[h], answer_hbm.at[h])
     folds = []
     for h in range(heads):
@@ -353,7 +355,7 @@
         cols = slice(g * DK, (g + 1) * DK)
         q = conv(rim_ref[:, cols], q_ref[:, cols], qt_ref[:, cols])
         queries.append(q)
-        cross.append(dot(q.astype(BF16), keys_ref[:, cols], NT))
+        cross.append(dot3(split(q), [keys_ref[i, :, cols] for i in range(2)], NT))
     spans = (slice(0, side), slice(side, rows))
     for h in range(heads):
         g = h // ratio
@@ -362,10 +364,11 @@
         for i, j in ((0, 0), (1, 0), (1, 1)):
             spread = upto_col[spans[i], h : h + 1] - upto_row[h : h + 1, spans[j]]
             value = jnp.exp(jnp.minimum(spread, 0.0)) * cross[g][spans[i], spans[j]]
-            sims[i, j] = (jnp.where(lower, value, 0.0) if i == j else value).astype(BF16)
+            sims[i, j] = split(jnp.where(lower, value, 0.0) if i == j else value)
         for i in range(2):
-            left = sims[0, 0] if i == 0 else jnp.concatenate([sims[1, 0], sims[1, 1]], axis=1)
-            emitted = dot(left, answer_ref[h, : left.shape[1]])
+            left = sims[0, 0] if i == 0 else [jnp.concatenate([sims[1, 0][p], sims[1, 1][p]], axis=1) for p in range(2)]
+            width = left[0].shape[1]
+            emitted = dot3(left, [answer_ref[h, p, :width] for p in range(2)])
             base_ref[spans[i], vcols] = emitted[:, DK:]
             gone = jnp.exp(upto_col[spans[i], h : h + 1])
             reach_ref[spans[i], vcols] = (gone * queries[g][spans[i]] - emitted[:, :DK]).astype(BF16)
@@ -488,8 +491,8 @@
     inputs = (rim_rows, *small, *early, key_in, value_in)
     made = (
         shape((2 * heads, DK + half, DK), BF16),
-        shape((heads, rows, DK + DV), BF16),
-        shape(key_in.shape, BF16),
+        shape((heads, 2, rows, DK + DV), BF16),
+        shape((2, *key_in.shape), BF16),
     )
     tops = (shape((rim, key_in.shape[1]), BF16), shape((rim, value_in.shape[1]), BF16))
     maps, answer, keys = call(

time: 95.2 us -> 95 us (level)
  no operation moved by 1% of the time
where the time goes in v4:
time: 95 us; the launch traced here: 94.6 us
  blocking collectives  56.5 us (59%)
  Pallas kernels  16.5 us (17%)
  starting transfers between devices  11.2 us (12%)
  waiting for transfers between devices  8.79 us (9%)
    all_to_all x1, blocking collectives, local(): lax.all_to_all(partial.reshape(ntp, rows // ntp, -1), 'tp', 0, 0, tiled=T...  24.4 us
    all_to_all x1, blocking collectives, local(): totals = lax.all_to_all(totals, 'z', 0, 0, tiled=True)  20.4 us
    pallas_call x7, Pallas kernels, call(): pl.pallas_call(kernel, out_shape=outs, in_specs=[far if i in hbm else vme...  16.5 us
    all_to_all x1, blocking collectives, local(): states = lax.all_to_all(states, 'y', 0, 0, tiled=True)  11.8 us
    all_to_all x1, waiting for transfers between devices, local(): maps = lax.all_to_all(maps, 'y', 0, 0, tiled=True)  8.79 us
    all_to_all x1, starting transfers between devices, local(): maps = lax.all_to_all(maps, 'y', 0, 0, tiled=True)  7.18 us
    ppermute x1, starting transfers between devices, local(): lax.ppermute(tail_rows, ('z', 'y'), [(i, i + 1) for i in range(count - 1)])  4.02 us
  transfers between devices with their start and end apart: 2, of which 1 were waited for; matrix products, arithmetic and copies ran while one was open for 0% of the time, Pallas kernels for 6%

profile of v4, /device:TPU:1, one launch (start us, length us, event | category | flops | bytes accessed | tf_op | source)
XLA Modules:
  0.0 94.6 jit_solution(4151058080656554025)
XLA Ops:
  0.0 1.4 %shard_map.109 = bf16[16,1024]{1,0:T(8,128)(2,1)} custom-call(bf16[256,256]{1,0:T(8,128)(2,1)} %q_ref.1, bf16[256,256]{1,0:T(8,128)(2,1)} %k_hbm.5, bf16[256,512]{1,0:T(8,128)(2,1)} %v_hbm.5), custom_call_target="tpu_custom_call" | custom-call | tf_op jit(solution)/shard_map/pallas_call | solution.py:429
  1.4 4.0 %collective-permute-start = (bf16[16,1024]{1,0:T(8,128)(2,1)}, bf16[16,1024]{1,0:T(8,128)(2,1)S(1)}, u32[]{:S(2)}, u32[]{:S(2)}) collective-permute-start(bf16[16,1024]{1,0:T(8,128)(2,1)} %shard_map.109), channel_id=1, source_target_pairs={{0,8},{8,16},{16,24},{24,32},{32,40},{40,48},{48,56},{56,64},{64,7... | collective-permute-start | bytes 98312 | tf_op jit(solution)/shard_map/ppermute | solution.py:471
  5.4 2.5 %shard_map.110 = (f32[256,256]{1,0:T(8,128)}, f32[256,512]{1,0:T(8,128)}) custom-call(bf16[256,256]{1,0:T(8,128)(2,1)} %k_hbm.5, bf16[256,512]{1,0:T(8,128)(2,1)} %v_hbm.5, bf16[4,256]{1,0:T(4,128)(2,1)} %kt_hbm.3, bf16[4,512]{1,0:T(4,128)(2,1)} %vt_hbm.3), custom_call_target="tpu_custom_call" | custom-call | flops 100000000 | bytes 3145728 | tf_op jit(solution)/shard_map/pallas_call | solution.py:429
  7.9 0.0 collective-permute-done.rim_hbm.rim_ref
  7.9 0.0 copy-start.5
  8.0 0.6 copy-done.5
  8.6 5.8 %shard_map.111 = (bf16[8,192,128]{2,1,0:T(8,128)(2,1)}, bf16[4,2,256,256]{3,2,1,0:T(8,128)(2,1)}, bf16[2,256,256]{2,1,0:T(8,128)(2,1)}) custom-call(bf16[16,1024]{1,0:T(8,128)(2,1)} %copy-done.5, bf16[4,256]{1,0:T(4,128)(2,1)} %kt_hbm.3, bf16[4,512]{1,0:T(4,128)(2,1)} %vt_hbm.3, f32[4,256]{1,0:T(4,128)} %beta_hbm.1, f32[4,256]{1,0:T(4,128)} %decay_ref.1, ...), custom_call_target="tpu_custom_call" | custom-call | tf_op jit(solution)/shard_map/pallas_call | solution.py:429
  14.4 7.2 %all-to-all-start = ((bf16[8,192,128]{2,1,0:T(8,128)(2,1)}), bf16[8,192,128]{2,1,0:T(8,128)(2,1)S(1)}, u32[]{:S(2)}, u32[]{:S(2)}) async-start(bf16[8,192,128]{2,1,0:T(8,128)(2,1)} %get-tuple-element.19), calls=%async_computation | async-start | bytes 786432 | tf_op jit(solution)/shard_map/all_to_all | solution.py:522
  21.5 0.0 copy-start
  21.6 0.0 copy-start.2
  21.6 0.0 copy-start.4
  21.6 3.5 %shard_map.112 = (f32[256,512]{1,0:T(8,128)}, bf16[256,512]{1,0:T(8,128)(2,1)}) custom-call(bf16[16,1024]{1,0:T(8,128)(2,1)} %copy-done.5, bf16[256,256]{1,0:T(8,128)(2,1)} %q_ref.1, bf16[4,256]{1,0:T(4,128)(2,1)} %qt_ref.1, f32[4,256]{1,0:T(4,128)} %decay_ref.1, bf16[4,2,256,256]{3,2,1,0:T(8,128)(2,1)} %get-tuple-element.20.answer_ref, ...), custom_call_target="tpu_custom_call" | custom-call | tf_op jit(solution)/shard_map/pallas_call | solution.py:429
  25.1 0.0 copy-start.1
  25.1 0.0 copy-start.3
  25.1 8.8 %all-to-all-done.maps_ref = bf16[8,192,128]{2,1,0:T(8,128)(2,1)S(1)} async-done(((bf16[8,192,128]{2,1,0:T(8,128)(2,1)}), bf16[8,192,128]{2,1,0:T(8,128)(2,1)S(1)}, u32[]{:S(2)}, u32[]{:S(2)}) %all-to-all-start) | async-done | bytes 393248 | tf_op jit(solution)/shard_map/all_to_all | solution.py:522
  33.9 1.1 %shard_map.113 = (f32[8,192,128]{2,1,0:T(8,128)S(1)}, bf16[8,192,128]{2,1,0:T(8,128)(2,1)S(1)}) custom-call(bf16[8,192,128]{2,1,0:T(8,128)(2,1)S(1)} %all-to-all-done.maps_ref), custom_call_target="tpu_custom_call" | custom-call | tf_op jit(solution)/shard_map/pallas_call | solution.py:429
  35.0 20.4 %all_to_all.20.totals_ref = bf16[8,192,128]{2,1,0:T(8,128)(2,1)S(1)} all-to-all(bf16[8,192,128]{2,1,0:T(8,128)(2,1)S(1)} %get-tuple-element.27), channel_id=1, replica_groups=mesh['z'=8,'y'=8,'tp'=8] {'z'}, dimensions={0} | all-to-all | bytes 786432 | tf_op jit(solution)/shard_map/all_to_all | solution.py:527
  55.4 1.2 %shard_map.114 = bf16[8,64,128]{2,1,0:T(8,128)(2,1)S(1)} custom-call(bf16[8,192,128]{2,1,0:T(8,128)(2,1)S(1)} %all_to_all.20.totals_ref, f32[8,192,128]{2,1,0:T(8,128)S(1)} %get-tuple-element.28.prefix_ref), custom_call_target="tpu_custom_call" | custom-call | tf_op jit(solution)/shard_map/pallas_call | solution.py:429
  56.5 11.8 %all_to_all.21 = bf16[8,64,128]{2,1,0:T(8,128)(2,1)S(1)} all-to-all(bf16[8,64,128]{2,1,0:T(8,128)(2,1)S(1)} %shard_map.114), channel_id=1, replica_groups=mesh['z'=8,'y'=8,'tp'=8] {'y'}, dimensions={0} | all-to-all | bytes 262144 | tf_op jit(solution)/shard_map/all_to_all | solution.py:529
  68.3 0.0 copy-done
  68.3 0.0 copy-done.2
  68.3 0.0 copy-done.4
  68.3 0.0 copy-done.1
  68.3 0.0 copy-done.3
  68.3 1.1 %shard_map.115 = bf16[256,2048]{1,0:T(8,128)(2,1)S(1)} custom-call(f32[256,512]{1,0:T(8,128)S(1)} %copy-done.1, bf16[256,512]{1,0:T(8,128)(2,1)S(1)} %copy-done.3, bf16[4,128,128]{2,1,0:T(8,128)(2,1)S(1)} %bitcast.4, bf16[256,512]{1,0:T(8,128)(2,1)S(1)} %copy-done.2, f32[1,128]{1,0:T(1,128)S(1)} %bitcast.5, bf16[512,2048]{1,0:T(8,128)(2,1)S(1)} %copy-done), custom_call_target="tpu_custom_call" | custom-call | tf_op jit(solution)/shard_map/pallas_call | solution.py:429
  69.4 24.4 %all_to_all.22 = bf16[8,32,2048]{2,1,0:T(8,128)(2,1)S(1)} all-to-all(bf16[8,32,2048]{2,1,0:T(8,128)(2,1)S(1)} %bitcast.3), channel_id=1, replica_groups=mesh['z'=8,'y'=8,'tp'=8] {'tp'}, dimensions={0} | all-to-all | bytes 2097152 | tf_op jit(solution)/shard_map/all_to_all | solution.py:540
  93.7 0.8 reduce_sum.12
Async XLA Ops:
  1.4 6.5 %collective-permute-start = (bf16[16,1024]{1,0:T(8,128)(2,1)}, bf16[16,1024]{1,0:T(8,128)(2,1)S(1)}, u32[]{:S(2)}, u32[]{:S(2)}) collective-permute-start(bf16[16,1024]{1,0:T(8,128)(2,1)} %shard_map.109), channel_id=1, source_target_pairs={{0,8},{8,16},{16,24},{24,32},{32,40},{40,48},{48,56},{56,64},{64,7... | collective-permute-start | bytes 98312 | tf_op jit(solution)/shard_map/ppermute | solution.py:471
  7.9 0.6 copy-start.5
  14.4 19.5 %all-to-all-start = ((bf16[8,192,128]{2,1,0:T(8,128)(2,1)}), bf16[8,192,128]{2,1,0:T(8,128)(2,1)S(1)}, u32[]{:S(2)}, u32[]{:S(2)}) async-start(bf16[8,192,128]{2,1,0:T(8,128)(2,1)} %get-tuple-element.19), calls=%async_computation | async-start | bytes 786432 | tf_op jit(solution)/shard_map/all_to_all | solution.py:522
  21.5 46.7 %copy-start = (bf16[512,2048]{1,0:T(8,128)(2,1)S(1)}, bf16[512,2048]{1,0:T(8,128)(2,1)}, u32[]{:S(2)}) copy-start(bf16[512,2048]{1,0:T(8,128)(2,1)} %weight_ref.1) | copy-start | bytes 6291460
  21.6 46.7 %copy-start.2 = (bf16[256,512]{1,0:T(8,128)(2,1)S(1)}, bf16[256,512]{1,0:T(8,128)(2,1)}, u32[]{:S(2)}) copy-start(bf16[256,512]{1,0:T(8,128)(2,1)} %gate_ref.1) | copy-start | bytes 786436
  21.6 46.7 %copy-start.4 = (f32[128]{0:T(128)S(1)}, f32[128]{0:T(128)}, u32[]{:S(2)}) copy-start(f32[128]{0:T(128)} %param.20) | copy-start | bytes 1540
  25.1 43.2 %copy-start.1 = (f32[256,512]{1,0:T(8,128)S(1)}, f32[256,512]{1,0:T(8,128)}, u32[]{:S(2)}) copy-start(f32[256,512]{1,0:T(8,128)} %get-tuple-element.24.base_ref) | copy-start | bytes 1572868
  25.1 43.2 %copy-start.3 = (bf16[256,512]{1,0:T(8,128)(2,1)S(1)}, bf16[256,512]{1,0:T(8,128)(2,1)}, u32[]{:S(2)}) copy-start(bf16[256,512]{1,0:T(8,128)(2,1)} %get-tuple-element.25.reach_ref) | copy-start | bytes 786436
